TPU v7x, 128 devices: a whole 4x4x4 slice. The times are simulated.
128 devices in a mesh: pts: 64 (over z, y_hi, x, core), rep: 2 (over y_lo).
Axes of the slice: x: 4, y: 4 (y_hi: 2, y_lo: 2; y = y_hi * 2 + y_lo), z: 4, core: 2. Of those that a mesh axis runs over, the one named last changes fastest.
Arguments:
- points: bfloat16 [262144, 512], P(('rep', 'pts')), parts along dimension 0, may hold values from -6 to 6
- point_row_index: int32 [262144], P(('rep', 'pts')), parts along dimension 0, may hold values from 0 to 131071, as said below
- neighbour_ball_list: int32 [1024, 4], P(('rep', 'pts')), parts along dimension 0, may hold values from 0 to 511, as said below
- attention_norm_gain: float32 [512], replicated, may hold values from 0.1 to 1.9
- query_weight: bfloat16 [512, 512], replicated, may hold values from -0.25 to 0.25
- key_weight: bfloat16 [512, 512], replicated, may hold values from -0.25 to 0.25
- value_weight: bfloat16 [512, 512], replicated, may hold values from -0.25 to 0.25
- pooled_key_weight: bfloat16 [512, 512], replicated, may hold values from -0.75 to 0.75
- pooled_value_weight: bfloat16 [512, 512], replicated, may hold values from -0.75 to 0.75
- head_score_scale: float32 [16], replicated, may hold values from 4 to 16
- output_weight: bfloat16 [512, 512], replicated, may hold values from -0.25 to 0.25
- feedforward_norm_gain: float32 [512], replicated, may hold values from 0.1 to 1.9
- gate_weight: bfloat16 [512, 1024], replicated, may hold values from -0.25 to 0.25
- up_weight: bfloat16 [512, 1024], replicated, may hold values from -0.25 to 0.25
- down_weight: bfloat16 [1024, 512], replicated, may hold values from -0.1875 to 0.1875
Outputs:
- layer_out: bfloat16 [262144, 512], P(('rep', 'pts')), parts along dimension 0
There are 2 independent parts, one for each index of `rep`. A program takes and returns all parts, laid end to end along the dimension named above; an argument that names none is the same for every part. Nothing has to cross between parts.
Inputs may be any that keep to these rules, and one draw needn't show every extreme that they name: point_row_index holds every number of 0 to 131071 once; of the 2048 points of one device (rows d * 2048 to (d + 1) * 2048 - 1 of points) exactly 32 go to the rows of each device. `neighbour_ball_list`: row b starts with b itself; its other three entries are balls on three different devices among those 1 to 4 places away from ball b's device around the loop of devices, ball c lying on device c // 8.
All inputs are finite; a program needn't handle non-finite values.
Results may differ from a plain program's by a relative error of at most 0.012.
Values may be sent and summed in bfloat16 or wider, within the bound.
A program may use at most 128 MiB of HBM per device.

v0:
```python
import jax
import jax.numpy as jnp
from jax import lax
from jax.sharding import PartitionSpec as P

BALL = 256
POOL = 8
OWNERS = 4
REACH = 4


def from_behind(block, axis, distance):
    devices = range(lax.axis_size(axis))
    route = [((i - distance) % len(devices), i) for i in devices]
    return lax.ppermute(block, axis, route)


def row_norm(values, scale_gain):
    mean_square = jnp.mean(values * values, axis=-1, keepdims=True)
    return values * lax.rsqrt(mean_square + 1e-05) * scale_gain


def head_norm(values, head_total):
    shaped = values.reshape(values.shape[0], head_total, -1)
    mean_square = jnp.mean(shaped * shaped, axis=-1, keepdims=True)
    return shaped * lax.rsqrt(mean_square + 1e-06)


def column_head_norm(values):
    mean_square = jnp.mean(values * values, axis=1, keepdims=True)
    return values * lax.rsqrt(mean_square + 1e-06)


def project_columns(rows, weight):
    return jnp.einsum("nc,cx->xn", rows, weight, preferred_element_type=jnp.float32)


def fetch_blocks(payload):
    both_sides = []
    for step_sign in (1, -1):
        received = [payload]
        received.append(from_behind(payload, "pts", step_sign))
        for places in range(2, REACH + 1):
            received.append(from_behind(payload, "pts", step_sign * places))
        both_sides.append(received)
    upward = both_sides[0]
    downward = both_sides[1]
    ordered = (
        [upward[k] for k in range(REACH, 0, -1)]
        + [payload]
        + [downward[k] for k in range(1, REACH + 1)]
    )
    return jnp.stack(ordered)


def on_device(
    points,
    point_row_index,
    neighbour_ball_list,
    attention_norm_gain,
    query_weight,
    key_weight,
    value_weight,
    pooled_key_weight,
    pooled_value_weight,
    head_score_scale,
    output_weight,
    feedforward_norm_gain,
    gate_weight,
    up_weight,
    down_weight,
):
    rows_dev, model_width = points.shape
    head_total = head_score_scale.shape[0]
    head_size = model_width // head_total
    peer_count = lax.axis_size("pts")
    my_index = lax.axis_index("pts")
    send_each = rows_dev // peer_count
    blocks_dev = rows_dev // BALL
    comp_rows = BALL // POOL
    sort_order = jnp.argsort(point_row_index)
    outgoing = jnp.take(points, sort_order, axis=0).reshape(peer_count, send_each, model_width)
    outgoing_ids = jnp.take(point_row_index, sort_order, axis=0).reshape(peer_count, send_each)
    arrived, arrived_ids = (
        lax.all_to_all(outgoing, "pts", split_axis=0, concat_axis=0, tiled=True),
        lax.all_to_all(outgoing_ids, "pts", split_axis=0, concat_axis=0, tiled=True),
    )
    local_slots = arrived_ids.reshape(rows_dev) - my_index * rows_dev
    grouped = jnp.take(arrived.reshape(rows_dev, model_width), jnp.argsort(local_slots), axis=0)
    normed = row_norm(grouped.astype(jnp.float32), attention_norm_gain).astype(jnp.bfloat16)
    col_shape = (head_total, head_size, rows_dev)
    query_cols = column_head_norm(project_columns(normed, query_weight).reshape(col_shape)).astype(
        jnp.bfloat16
    )
    key_cols = column_head_norm(project_columns(normed, key_weight).reshape(col_shape)).astype(
        jnp.bfloat16
    )
    value_cols = project_columns(normed, value_weight).astype(jnp.bfloat16).reshape(col_shape)
    pooled = jnp.mean(
        normed.astype(jnp.float32).reshape(rows_dev // POOL, POOL, model_width), axis=1
    ).astype(jnp.bfloat16)
    comp_key = head_norm(
        jnp.dot(pooled, pooled_key_weight, preferred_element_type=jnp.float32), head_total
    )
    comp_key = comp_key.astype(jnp.bfloat16).reshape(blocks_dev * comp_rows, model_width)
    comp_value = jnp.dot(pooled, pooled_value_weight, preferred_element_type=jnp.float32).astype(
        jnp.bfloat16
    )
    payload = jnp.concatenate([comp_key, comp_value], axis=1)
    payload_width = payload.shape[1]
    candidates = fetch_blocks(payload).reshape(
        (2 * REACH + 1) * blocks_dev, comp_rows, payload_width
    )
    owner_device = neighbour_ball_list // blocks_dev
    offsets = jnp.mod(owner_device - my_index + REACH, peer_count) - REACH
    chosen_rows = (offsets + REACH) * blocks_dev + neighbour_ball_list % blocks_dev
    chosen = jnp.take(candidates, chosen_rows.reshape(-1), axis=0).reshape(
        blocks_dev, OWNERS * comp_rows, payload_width
    )
    score_scale = (head_score_scale / head_size)[:, None, None]
    output_heads = output_weight.reshape(head_total, head_size, model_width)
    coarse_count = OWNERS * comp_rows

    def one_ball(ball_index):
        start = ball_index * BALL
        ball_query = lax.dynamic_slice_in_dim(query_cols, start, BALL, 2)
        ball_key = lax.dynamic_slice_in_dim(key_cols, start, BALL, 2)
        ball_value = lax.dynamic_slice_in_dim(value_cols, start, BALL, 2)
        coarse = lax.dynamic_index_in_dim(chosen, ball_index, 0, keepdims=False)
        coarse_key = coarse[:, :model_width].T.reshape(head_total, head_size, coarse_count)
        coarse_value = coarse[:, model_width:].T.reshape(head_total, head_size, coarse_count)
        local_score = (
            jnp.einsum("hdq,hdk->hqk", ball_query, ball_key, preferred_element_type=jnp.float32)
            * score_scale
        )
        far_score = (
            jnp.einsum("hdq,hdk->hqk", ball_query, coarse_key, preferred_element_type=jnp.float32)
            * score_scale
        )
        local_exp = jnp.exp(local_score)
        far_exp = jnp.exp(far_score)
        denominator = jnp.sum(local_exp, axis=-1, keepdims=True) + jnp.sum(
            far_exp, axis=-1, keepdims=True
        )
        local_prob = (local_exp / denominator).astype(jnp.bfloat16)
        far_prob = (far_exp / denominator).astype(jnp.bfloat16)
        attended = jnp.einsum(
            "hqk,hdk->hdq", local_prob, ball_value, preferred_element_type=jnp.float32
        )
        attended = attended + jnp.einsum(
            "hqk,hdk->hdq", far_prob, coarse_value, preferred_element_type=jnp.float32
        )
        attended = attended.astype(jnp.bfloat16)
        return jnp.einsum("hdq,hde->qe", attended, output_heads, preferred_element_type=jnp.float32)

    projected_rows = lax.map(one_ball, jnp.arange(blocks_dev, dtype=jnp.int32)).reshape(
        rows_dev, model_width
    )
    residual = (grouped.astype(jnp.float32) + projected_rows).astype(jnp.bfloat16)
    ffn_normed = row_norm(residual.astype(jnp.float32), feedforward_norm_gain).astype(jnp.bfloat16)
    gate_proj = jnp.dot(ffn_normed, gate_weight, preferred_element_type=jnp.float32)
    up_proj = jnp.dot(ffn_normed, up_weight, preferred_element_type=jnp.float32)
    hidden = (jax.nn.silu(gate_proj) * up_proj).astype(jnp.bfloat16)
    ball_out = (
        residual.astype(jnp.float32)
        + jnp.dot(hidden, down_weight, preferred_element_type=jnp.float32)
    ).astype(jnp.bfloat16)
    returning = jnp.take(ball_out, local_slots, axis=0).reshape(peer_count, send_each, model_width)
    came_back = lax.all_to_all(returning, "pts", split_axis=0, concat_axis=0, tiled=True).reshape(
        rows_dev, model_width
    )
    return jnp.take(came_back, jnp.argsort(sort_order), axis=0)


def solution(mesh):
    return jax.shard_map(
        on_device,
        mesh=mesh,
        in_specs=(
            P(("rep", "pts"), None),
            P(("rep", "pts")),
            P(("rep", "pts"), None),
            P(),
            P(),
            P(),
            P(),
            P(),
            P(),
            P(),
            P(),
            P(),
            P(),
            P(),
            P(),
        ),
        out_specs=P(("rep", "pts"), None),
        check_vma=False,
    )
```

profile of v0, /device:TPU:1, one launch (start us, length us, event | category | flops | bytes accessed | tf_op | source)
XLA Modules:
  0.0 366.2 jit_solution(11641468990507260605)
XLA Ops:
  0.0 5.9 %sort.45 = (s32[2048]{0:T(1024)}, s32[2048]{0:T(1024)S(1)}) sort(s32[2048]{0:T(1024)} %param.20, s32[2048]{0:T(1024)S(1)} %iota.13), dimensions={0}, to_apply=%region_0.0 | sort | flops 22528 | bytes 32768 | tf_op jit(solution)/shard_map/jit(argsort)/sort | solution.py:81
  5.9 11.8 %gather_fusion = s32[2048]{0:T(1024)S(1)} fusion(s32[2048]{0:T(1024)S(1)} %copy-done.2, s32[2048]{0:T(1024)S(1)} %fusion.29), kind=kCustom, calls=%fused_computation.4 | custom fusion | bytes 24576 | tf_op jit(solution)/shard_map/jit(_take)/gather | solution.py:83
  18.4 12.5 %all-to-all-start.1 = ((s32[64,1,32]{2,1,0:T(1,128)}), s32[64,1,32]{2,1,0:T(1,128)S(1)}, u32[]{:S(2)}, u32[]{:S(2)}) async-start(s32[64,1,32]{2,1,0:T(1,128)} %bitcast.9), calls=%async_computation.1 | async-start | bytes 65536 | tf_op jit(solution)/shard_map/all_to_all | solution.py:86
  30.9 9.2 %gather_fusion.2 = bf16[2048,512]{1,0:T(8,128)(2,1)} fusion(bf16[2048,512]{1,0:T(8,128)(2,1)S(1)} %copy-done, s32[2048]{0:T(1024)S(1)} %fusion.29), kind=kCustom, calls=%fused_computation.clone | custom fusion | bytes 4202496 | tf_op jit(solution)/shard_map/jit(_take)/gather | solution.py:82
  42.9 10.3 %all-to-all-start = ((bf16[64,32,512]{2,1,0:T(8,128)(2,1)}), bf16[64,32,512]{2,1,0:T(8,128)(2,1)S(1)}, u32[]{:S(2)}, u32[]{:S(2)}) async-start(bf16[64,32,512]{2,1,0:T(8,128)(2,1)} %bitcast.101), calls=%async_computation | async-start | bytes 4194304 | tf_op jit(solution)/shard_map/all_to_all | solution.py:85
  53.9 5.0 %sort.46 = (s32[2048]{0:T(1024)}, s32[2048]{0:T(1024)S(1)}) sort(s32[2048]{0:T(1024)S(1)} %sub.24, s32[2048]{0:T(1024)S(1)} %iota.14), dimensions={0}, to_apply=%region_1.3 | sort | flops 22528 | bytes 32768 | tf_op jit(solution)/shard_map/jit(argsort)/sort | solution.py:89
  59.0 25.0 %all-to-all-done = bf16[64,32,512]{2,1,0:T(8,128)(2,1)S(1)} async-done(((bf16[64,32,512]{2,1,0:T(8,128)(2,1)}), bf16[64,32,512]{2,1,0:T(8,128)(2,1)S(1)}, u32[]{:S(2)}, u32[]{:S(2)}) %all-to-all-start) | async-done | bytes 2097184 | tf_op jit(solution)/shard_map/all_to_all | solution.py:85
  84.0 9.2 %gather_fusion.3 = bf16[2048,512]{1,0:T(8,128)(2,1)} fusion(bf16[2048,512]{1,0:T(8,128)(2,1)S(1)} %bitcast.97, s32[2048]{0:T(1024)S(1)} %fusion.30), kind=kCustom, calls=%fused_computation.1.clone | custom fusion | bytes 4202496 | tf_op jit(solution)/shard_map/jit(_take)/gather | solution.py:89
  95.6 3.4 convert_reduce_fusion
  115.2 3.4 multiply_convert_fusion.1
  118.6 3.2 convolution_convert_fusion
  121.8 4.1 %collective-permute-done = bf16[256,1024]{1,0:T(8,128)(2,1)S(1)} collective-permute-done((bf16[256,1024]{1,0:T(8,128)(2,1)S(1)}, bf16[256,1024]{1,0:T(8,128)(2,1)S(1)}, u32[]{:S(2)}, u32[]{:S(2)}) %collective-permute-start) | collective-permute-done | bytes 524320 | tf_op jit(solution)/shard_map/ppermute | solution.py:15
  128.3 14.4 %collective-permute-done.1 = bf16[256,1024]{1,0:T(8,128)(2,1)S(1)} collective-permute-done((bf16[256,1024]{1,0:T(8,128)(2,1)S(1)}, bf16[256,1024]{1,0:T(8,128)(2,1)S(1)}, u32[]{:S(2)}, u32[]{:S(2)}) %collective-permute-start.1) | collective-permute-done | bytes 524320 | tf_op jit(solution)/shard_map/ppermute | solution.py:15
  143.2 4.4 %collective-permute-start.7 = (bf16[256,1024]{1,0:T(8,128)(2,1)S(1)}, bf16[256,1024]{1,0:T(8,128)(2,1)S(1)}, u32[]{:S(2)}, u32[]{:S(2)}) collective-permute-start(bf16[256,1024]{1,0:T(8,128)(2,1)S(1)} %pad_maximum_fusion), channel_id=1, source_target_pairs={{8,0},{10,2},{12,4},{14,6},{16,8},{18,10},{20,12},{22,14},{24,16},... | collective-permute-start | bytes 1572872 | tf_op jit(solution)/shard_map/ppermute | solution.py:15
  150.2 8.5 %collective-permute-done.6 = bf16[256,1024]{1,0:T(8,128)(2,1)S(1)} collective-permute-done((bf16[256,1024]{1,0:T(8,128)(2,1)S(1)}, bf16[256,1024]{1,0:T(8,128)(2,1)S(1)}, u32[]{:S(2)}, u32[]{:S(2)}) %collective-permute-start.6) | collective-permute-done | bytes 524320 | tf_op jit(solution)/shard_map/ppermute | solution.py:15
  167.5 105.3 %while.10 = (s32[]{:T(128)}, f32[8,256,512]{2,1,0:T(8,128)}, s32[8]{0:T(128)S(1)}, bf16[16,32,2048]{2,1,0:T(8,128)(2,1)}, bf16[16,32,2048]{2,1,0:T(8,128)(2,1)},...) while((s32[]{:T(128)}, f32[8,256,512]{2,1,0:T(8,128)}, ...), condition=%wide.region_10.12_spmd, body=%wide.region_7.11_spmd.sunk | while | flops 343666688 | bytes 17680364 | solution.py:156
  272.8 3.5 fusion.20
  277.7 5.6 %fusion.26 = f32[2048,1024]{1,0:T(8,128)} fusion(bf16[512,1024]{1,0:T(8,128)(2,1)S(1)} %copy-done.9, bf16[2048,512]{1,0:T(8,128)(2,1)S(1)} %get-tuple-element.97, f32[512]{0:T(512)S(1)} %copy-done.14, f32[2048]{0:T(1024)S(1)} %add_rsqrt_fusion.3), kind=kOutput, calls=%fused_computation.55 | convolution fusion | flops 2151677952 | bytes 11544576 | tf_op jit(solution)/shard_map/dot_general | solution.py:161
  283.3 9.8 %fusion.23 = bf16[2048,512]{1,0:T(8,128)(2,1)S(1)} fusion(bf16[2048,512]{1,0:T(8,128)(2,1)} %copy-done.4, bf16[1024,512]{1,0:T(8,128)(2,1)S(1)} %copy-done.10, f32[2048,1024]{1,0:T(8,128)} %fusion.26, bf16[512,1024]{1,0:T(8,128)(2,1)} %param.32, f32[512]{0:T(512)S(1)} %copy-done.14, f32[2048]{0:T(1024)S(1)} %add_rsqrt_fusion.3), kind=kOutput, calls=%fused_computation.42 | convolution fusion | flops 4314890240 | bytes 14690304 | tf_op jit(solution)/shard_map/dot_general | solution.py:166
  293.1 9.2 %gather_fusion.4 = bf16[2048,512]{1,0:T(8,128)(2,1)} fusion(bf16[2048,512]{1,0:T(8,128)(2,1)S(1)} %fusion.23, s32[2048]{0:T(1024)S(1)} %fusion.31), kind=kCustom, calls=%fused_computation.2.clone | custom fusion | bytes 4202496 | tf_op jit(solution)/shard_map/jit(_take)/gather | solution.py:168
  305.1 16.3 %all-to-all-start.2 = ((bf16[64,32,512]{2,1,0:T(8,128)(2,1)}), bf16[64,32,512]{2,1,0:T(8,128)(2,1)}, u32[]{:S(2)}, u32[]{:S(2)}) async-start(bf16[64,32,512]{2,1,0:T(8,128)(2,1)} %bitcast.38), calls=%async_computation.2 | async-start | bytes 4194304 | tf_op jit(solution)/shard_map/all_to_all | solution.py:169
  321.4 5.0 %sort.47 = (s32[2048]{0:T(1024)}, s32[2048]{0:T(1024)S(1)}) sort(s32[2048]{0:T(1024)S(1)} %get-tuple-element.56, s32[2048]{0:T(1024)S(1)} %iota.16), dimensions={0}, to_apply=%region_12.14 | sort | flops 22528 | bytes 32768 | tf_op jit(solution)/shard_map/jit(argsort)/sort | solution.py:172
  326.4 25.7 %all-to-all-done.2 = bf16[64,32,512]{2,1,0:T(8,128)(2,1)} async-done(((bf16[64,32,512]{2,1,0:T(8,128)(2,1)}), bf16[64,32,512]{2,1,0:T(8,128)(2,1)}, u32[]{:S(2)}, u32[]{:S(2)}) %all-to-all-start.2) | async-done | bytes 2097184 | tf_op jit(solution)/shard_map/all_to_all | solution.py:169
  352.1 11.3 %gather_fusion.5 = bf16[2048,512]{1,0:T(8,128)(2,1)} fusion(bf16[2048,512]{1,0:T(8,128)(2,1)} %bitcast.39, s32[2048]{0:T(1024)S(1)} %fusion.32), kind=kCustom, calls=%fused_computation.3.clone | custom fusion | bytes 4202496 | tf_op jit(solution)/shard_map/jit(_take)/gather | solution.py:172
  (172 shorter events, 128.7 us)
Async XLA Ops:
  0.0 30.9 %copy-start = (bf16[2048,512]{1,0:T(8,128)(2,1)S(1)}, bf16[2048,512]{1,0:T(8,128)(2,1)}, u32[]{:S(2)}) copy-start(bf16[2048,512]{1,0:T(8,128)(2,1)} %param.19) | copy-start | bytes 6291460
  0.0 5.9 %copy-start.2 = (s32[2048]{0:T(1024)S(1)}, s32[2048]{0:T(1024)}, u32[]{:S(2)}) copy-start(s32[2048]{0:T(1024)} %param.20) | copy-start | bytes 24580
  18.4 24.5 %all-to-all-start.1 = ((s32[64,1,32]{2,1,0:T(1,128)}), s32[64,1,32]{2,1,0:T(1,128)S(1)}, u32[]{:S(2)}, u32[]{:S(2)}) async-start(s32[64,1,32]{2,1,0:T(1,128)} %bitcast.9), calls=%async_computation.1 | async-start | bytes 65536 | tf_op jit(solution)/shard_map/all_to_all | solution.py:86
  40.1 13.2 %copy-start.8 = (s32[8,4]{0,1:T(4,128)S(1)}, s32[8,4]{0,1:T(4,128)}, u32[]{:S(2)}) copy-start(s32[8,4]{0,1:T(4,128)} %param.21) | copy-start | bytes 388
  40.1 13.6 %copy-start.15 = (f32[16]{0:T(128)S(1)}, f32[16]{0:T(128)}, u32[]{:S(2)}) copy-start(f32[16]{0:T(128)} %param.28) | copy-start | bytes 196
  42.9 41.2 %all-to-all-start = ((bf16[64,32,512]{2,1,0:T(8,128)(2,1)}), bf16[64,32,512]{2,1,0:T(8,128)(2,1)S(1)}, u32[]{:S(2)}, u32[]{:S(2)}) async-start(bf16[64,32,512]{2,1,0:T(8,128)(2,1)} %bitcast.101), calls=%async_computation | async-start | bytes 4194304 | tf_op jit(solution)/shard_map/all_to_all | solution.py:85
  84.0 11.5 %copy-start.7 = (f32[512]{0:T(512)S(1)}, f32[512]{0:T(512)}, u32[]{:S(2)}) copy-start(f32[512]{0:T(512)} %param.22) | copy-start | bytes 6148
  93.2 5.7 %copy-start.6 = (bf16[512,512]{1,0:T(8,128)(2,1)S(1)}, bf16[512,512]{1,0:T(8,128)(2,1)}, u32[]{:S(2)}) copy-start(bf16[512,512]{1,0:T(8,128)(2,1)} %param.26) | copy-start | bytes 1572868
  99.0 11.5 %copy-start.3 = (bf16[2048,512]{1,0:T(8,128)(2,1)S(1)}, bf16[2048,512]{1,0:T(8,128)(2,1)}, u32[]{:S(2)}) copy-start(bf16[2048,512]{1,0:T(8,128)(2,1)} %gather_fusion.3) | copy-start | bytes 6291460
  106.2 7.1 %copy-start.11 = (bf16[512,512]{1,0:T(8,128)(2,1)S(1)}, bf16[512,512]{1,0:T(8,128)(2,1)}, u32[]{:S(2)}) copy-start(bf16[512,512]{1,0:T(8,128)(2,1)} %param.24) | copy-start | bytes 1572868
  106.3 19.6 %collective-permute-start = (bf16[256,1024]{1,0:T(8,128)(2,1)S(1)}, bf16[256,1024]{1,0:T(8,128)(2,1)S(1)}, u32[]{:S(2)}, u32[]{:S(2)}) collective-permute-start(bf16[256,1024]{1,0:T(8,128)(2,1)S(1)} %pad_maximum_fusion), channel_id=1, source_target_pairs={{120,0},{122,2},{124,4},{126,6},{0,8},{2,10},{4,12},{6,14},{8,16},... | collective-permute-start | bytes 1572872 | tf_op jit(solution)/shard_map/ppermute | solution.py:15
  106.3 36.4 %collective-permute-start.1 = (bf16[256,1024]{1,0:T(8,128)(2,1)S(1)}, bf16[256,1024]{1,0:T(8,128)(2,1)S(1)}, u32[]{:S(2)}, u32[]{:S(2)}) collective-permute-start(bf16[256,1024]{1,0:T(8,128)(2,1)S(1)} %pad_maximum_fusion), channel_id=1, source_target_pairs={{122,0},{124,2},{126,4},{0,6},{2,8},{4,10},{6,12},{8,14},{10,16},{... | collective-permute-start | bytes 1572872 | tf_op jit(solution)/shard_map/ppermute | solution.py:15
  109.2 34.0 %collective-permute-start.2 = (bf16[256,1024]{1,0:T(8,128)(2,1)S(1)}, bf16[256,1024]{1,0:T(8,128)(2,1)S(1)}, u32[]{:S(2)}, u32[]{:S(2)}) collective-permute-start(bf16[256,1024]{1,0:T(8,128)(2,1)S(1)} %pad_maximum_fusion), channel_id=1, source_target_pairs={{124,0},{126,2},{0,4},{2,6},{4,8},{6,10},{8,12},{10,14},{12,16},{1... | collective-permute-start | bytes 1572872 | tf_op jit(solution)/shard_map/ppermute | solution.py:15
  109.9 40.1 %collective-permute-start.3 = (bf16[256,1024]{1,0:T(8,128)(2,1)S(1)}, bf16[256,1024]{1,0:T(8,128)(2,1)S(1)}, u32[]{:S(2)}, u32[]{:S(2)}) collective-permute-start(bf16[256,1024]{1,0:T(8,128)(2,1)S(1)} %pad_maximum_fusion), channel_id=1, source_target_pairs={{126,0},{0,2},{2,4},{4,6},{6,8},{8,10},{10,12},{12,14},{14,16},{16... | collective-permute-start | bytes 1572872 | tf_op jit(solution)/shard_map/ppermute | solution.py:15
  109.9 40.2 %collective-permute-start.4 = (bf16[256,1024]{1,0:T(8,128)(2,1)S(1)}, bf16[256,1024]{1,0:T(8,128)(2,1)S(1)}, u32[]{:S(2)}, u32[]{:S(2)}) collective-permute-start(bf16[256,1024]{1,0:T(8,128)(2,1)S(1)} %pad_maximum_fusion), channel_id=1, source_target_pairs={{2,0},{4,2},{6,4},{8,6},{10,8},{12,10},{14,12},{16,14},{18,16},{20... | collective-permute-start | bytes 1572872 | tf_op jit(solution)/shard_map/ppermute | solution.py:15
  125.9 24.3 %collective-permute-start.5 = (bf16[256,1024]{1,0:T(8,128)(2,1)S(1)}, bf16[256,1024]{1,0:T(8,128)(2,1)S(1)}, u32[]{:S(2)}, u32[]{:S(2)}) collective-permute-start(bf16[256,1024]{1,0:T(8,128)(2,1)S(1)} %pad_maximum_fusion), channel_id=1, source_target_pairs={{4,0},{6,2},{8,4},{10,6},{12,8},{14,10},{16,12},{18,14},{20,16},{2... | collective-permute-start | bytes 1572872 | tf_op jit(solution)/shard_map/ppermute | solution.py:15
  142.7 16.0 %collective-permute-start.6 = (bf16[256,1024]{1,0:T(8,128)(2,1)S(1)}, bf16[256,1024]{1,0:T(8,128)(2,1)S(1)}, u32[]{:S(2)}, u32[]{:S(2)}) collective-permute-start(bf16[256,1024]{1,0:T(8,128)(2,1)S(1)} %pad_maximum_fusion), channel_id=1, source_target_pairs={{6,0},{8,2},{10,4},{12,6},{14,8},{16,10},{18,12},{20,14},{22,16},{... | collective-permute-start | bytes 1572872 | tf_op jit(solution)/shard_map/ppermute | solution.py:15
  143.2 17.4 %collective-permute-start.7 = (bf16[256,1024]{1,0:T(8,128)(2,1)S(1)}, bf16[256,1024]{1,0:T(8,128)(2,1)S(1)}, u32[]{:S(2)}, u32[]{:S(2)}) collective-permute-start(bf16[256,1024]{1,0:T(8,128)(2,1)S(1)} %pad_maximum_fusion), channel_id=1, source_target_pairs={{8,0},{10,2},{12,4},{14,6},{16,8},{18,10},{20,12},{22,14},{24,16},... | collective-permute-start | bytes 1572872 | tf_op jit(solution)/shard_map/ppermute | solution.py:15
  162.8 4.7 %copy-start.13 = (bf16[512,512]{1,0:T(8,128)(2,1)S(1)}, bf16[512,512]{1,0:T(8,128)(2,1)}, u32[]{:S(2)}) copy-start(bf16[512,512]{1,0:T(8,128)(2,1)} %param.29) | copy-start | bytes 1572868
  272.8 4.9 %copy-start.9 = (bf16[512,1024]{1,0:T(8,128)(2,1)S(1)}, bf16[512,1024]{1,0:T(8,128)(2,1)}, u32[]{:S(2)}) copy-start(bf16[512,1024]{1,0:T(8,128)(2,1)} %param.31) | copy-start | bytes 3145732
  272.8 4.9 %copy-start.14 = (f32[512]{0:T(512)S(1)}, f32[512]{0:T(512)}, u32[]{:S(2)}) copy-start(f32[512]{0:T(512)} %param.30) | copy-start | bytes 6148
  277.6 5.6 %copy-start.10 = (bf16[1024,512]{1,0:T(8,128)(2,1)S(1)}, bf16[1024,512]{1,0:T(8,128)(2,1)}, u32[]{:S(2)}) copy-start(bf16[1024,512]{1,0:T(8,128)(2,1)} %param.33) | copy-start | bytes 3145732
  305.1 47.1 %all-to-all-start.2 = ((bf16[64,32,512]{2,1,0:T(8,128)(2,1)}), bf16[64,32,512]{2,1,0:T(8,128)(2,1)}, u32[]{:S(2)}, u32[]{:S(2)}) async-start(bf16[64,32,512]{2,1,0:T(8,128)(2,1)} %bitcast.38), calls=%async_computation.2 | async-start | bytes 4194304 | tf_op jit(solution)/shard_map/all_to_all | solution.py:169
  352.1 14.0 %copy-start.1 = (bf16[2048,512]{1,0:T(8,128)(2,1)S(1)}, bf16[2048,512]{1,0:T(8,128)(2,1)}, u32[]{:S(2)}) copy-start(bf16[2048,512]{1,0:T(8,128)(2,1)} %param.19) | copy-start | bytes 6291460
  (3 other events, 6.9 us)
where the time goes:
time: 368 us; the launch traced here: 366 us
  matrix products  97.1 us (26%)
  waiting for transfers between devices  82.4 us (22%)
  local copies, waits for them, and re-layouts  76 us (21%)
  starting transfers between devices  50.1 us (14%)
  other arithmetic  40.1 us (11%)
  loops' own time  20.1 us (5%)
    ppermute x8, waiting for transfers between devices, from_behind(): return lax.ppermute(block, axis, route)  31.7 us
    all_to_all x1, waiting for transfers between devices, on_device(): lax.all_to_all(returning, 'pts', split_axis=0, concat_axis=0, tiled=True)  25.7 us
    all_to_all x1, waiting for transfers between devices, on_device(): lax.all_to_all(outgoing, 'pts', split_axis=0, concat_axis=0, tiled=True)  25 us
    dot_general x8, matrix products, one_ball(): jnp.einsum('hdq,hde->qe', attended, output_heads, preferred_element_type=...  21.4 us
    dot_general x8, matrix products, one_ball(): jnp.einsum('hqk,hdk->hdq', local_prob, ball_value, preferred_element_type...  21 us
    another operation x1, loops' own time, on_device(): lax.map(one_ball, jnp.arange(blocks_dev, dtype=jnp.int32))  20.1 us
    dot_general x8, matrix products, one_ball(): jnp.einsum('hdq,hdk->hqk', ball_query, ball_key, preferred_element_type=j...  16.5 us
    all_to_all x1, starting transfers between devices, on_device(): lax.all_to_all(returning, 'pts', split_axis=0, concat_axis=0, tiled=True)  16.3 us
  transfers between devices with their start and end apart: 11, of which 8 were waited for; matrix products, arithmetic and copies ran while one was open for 9% of the time, Pallas kernels for 0%

commit v1 on v0

v1 whole, which is shorter than its diff:
```python
import functools
import math

import jax
import jax.numpy as jnp
from jax import lax
from jax.experimental import pallas as pl
from jax.experimental.pallas import tpu as pltpu
from jax.sharding import PartitionSpec as P

BALL = 256
POOL = 8
OWNERS = 4
REACH = 4
D = 512
HEADS = 16
HD = 32
FF = 1024
ROWS = 2048
PEERS = 64
EACH = 32
CK = BALL // POOL
KEYS = BALL + OWNERS * CK
GROUP = 8
NB = ROWS // BALL
MESH = pl.DeviceIdType.MESH
F32 = jnp.float32
BF16 = jnp.bfloat16
VMEM_LIMIT = 56 * 1024 * 1024


def vmem(n):
    return [pl.BlockSpec(memory_space=pltpu.VMEM)] * n


def fixed(shape):
    return pl.BlockSpec(shape, lambda *_: (0,) * len(shape), pipeline_mode=pl.Buffered(1))


def mm(a, b):
    return jnp.dot(a, b, preferred_element_type=F32)


def mm_nt(a, b):
    return lax.dot_general(a, b, (((1,), (1,)), ((), ())), preferred_element_type=F32)


def one_hot_rows(start, count, row):
    ids = lax.broadcasted_iota(jnp.int32, (count, ROWS), 0) + start
    return jnp.where(ids == row, 1.0, 0.0).astype(BF16)


def one_hot_cols(col, count):
    ids = lax.broadcasted_iota(jnp.int32, (count, ROWS), 1)
    return jnp.where(ids == col, 1.0, 0.0).astype(BF16)


def pack_kernel(col_ref, row_ref, x_ref, out_ref, ids_ref, pos_ref):
    step = pl.program_id(0)

    @pl.when(step == 0)
    def _():
        def count(j, acc):
            col = col_ref[pl.ds(pl.multiple_of(j * 256, 256), 256), :]
            less = jnp.where(col < row_ref[...], 1.0, 0.0)
            return acc + jnp.sum(less.reshape(32, 8, ROWS), axis=0)

        acc = lax.fori_loop(0, NB, count, jnp.zeros((8, ROWS), F32))
        pos_ref[...] = jnp.sum(acc, axis=0, keepdims=True).astype(jnp.int32)

    hot = one_hot_rows(step * 256, 256, pos_ref[...])
    out_ref[...] = mm(hot, x_ref[...]).astype(BF16)
    number = row_ref[...]
    high = (number // 2048).astype(F32)
    mid = ((number // 64) % 32).astype(F32)
    low = (number % 64).astype(F32)
    pad = jnp.zeros((5, ROWS), F32)
    parts = jnp.concatenate([high, mid, low, pad], axis=0).astype(BF16)
    back = mm_nt(parts, hot)
    whole = back[0:1] * 2048.0 + back[1:2] * 64.0 + back[2:3]
    whole = whole.astype(jnp.int32)
    ids_ref[0] = whole[:, :128]
    ids_ref[1] = whole[:, 128:]


def pack(col, row, x):
    return pl.pallas_call(
        pack_kernel,
        grid=(NB,),
        in_specs=[fixed((ROWS, 1)), fixed((1, ROWS)), fixed((ROWS, D))],
        out_specs=[
            pl.BlockSpec((256, D), lambda i: (i, 0)),
            pl.BlockSpec((2, 1, 128), lambda i: (i, 0, 0)),
            pl.BlockSpec((1, ROWS), lambda i: (0, 0)),
        ],
        out_shape=[
            jax.ShapeDtypeStruct((ROWS, D), BF16),
            jax.ShapeDtypeStruct((16, 1, 128), jnp.int32),
            jax.ShapeDtypeStruct((1, ROWS), jnp.int32),
        ],
        compiler_params=pltpu.CompilerParams(vmem_limit_bytes=VMEM_LIMIT),
        name="pack",
    )(col, row, x)


def peer(k):
    return lax.rem(lax.axis_index("pts") + k, PEERS)


def greet():
    barrier = pltpu.get_barrier_semaphore()

    def signal(k, carry):
        pl.semaphore_signal(barrier, inc=1, device_id={"pts": peer(k)}, device_id_type=MESH)
        return carry

    lax.fori_loop(1, PEERS, signal, 0)
    pl.semaphore_wait(barrier, PEERS - 1)


def exchange_kernel(with_ids, *refs):
    if with_ids:
        x_ref, i_ref, o_ref, oi_ref, send, recv, isend, irecv, here = refs
    else:
        x_ref, o_ref, send, recv, here = refs
    me = lax.axis_index("pts")
    greet()

    def rows(k):
        d = peer(k)
        return pltpu.make_async_remote_copy(
            src_ref=x_ref.at[d], dst_ref=o_ref.at[me], send_sem=send.at[k],
            recv_sem=recv.at[k], device_id={"pts": d}, device_id_type=MESH)

    def numbers(k):
        d = peer(k)
        return pltpu.make_async_remote_copy(
            src_ref=i_ref.at[d // 4], dst_ref=oi_ref.at[me], send_sem=isend.at[k],
            recv_sem=irecv.at[k], device_id={"pts": d}, device_id_type=MESH)

    def order(k):
        return lax.rem(k * 13, PEERS)

    def start(k, carry):
        rows(order(k)).start()
        if with_ids:
            numbers(order(k)).start()
        return carry

    def wait(k, carry):
        rows(k).wait()
        if with_ids:
            numbers(k).wait()
        return carry

    lax.fori_loop(1, PEERS, start, 0)
    own = pltpu.make_async_copy(x_ref.at[me], o_ref.at[me], here.at[0])
    own.start()
    if with_ids:
        own_ids = pltpu.make_async_copy(i_ref.at[me // 4], oi_ref.at[me], here.at[1])
        own_ids.start()
        own_ids.wait()
    own.wait()
    lax.fori_loop(1, PEERS, wait, 0)


def exchange(x, ids=None):
    with_ids = ids is not None
    shape = jax.ShapeDtypeStruct((PEERS, EACH, D), BF16)
    sems = [pltpu.SemaphoreType.DMA((PEERS,))] * (4 if with_ids else 2)
    sems = sems + [pltpu.SemaphoreType.DMA((2,))]
    args = (x.reshape(PEERS, EACH, D),)
    out_shape = shape
    out_specs = vmem(1)[0]
    if with_ids:
        args = args + (ids,)
        out_shape = [shape, jax.ShapeDtypeStruct((PEERS, 1, 128), jnp.int32)]
        out_specs = vmem(2)
    return pl.pallas_call(
        functools.partial(exchange_kernel, with_ids),
        in_specs=vmem(len(args)),
        out_specs=out_specs,
        out_shape=out_shape,
        scratch_shapes=sems,
        compiler_params=pltpu.CompilerParams(
            collective_id=0 if with_ids else 1, has_side_effects=True),
        name="exchange_ids" if with_ids else "exchange",
    )(*args)


def place_kernel(row_ref, x_ref, gain_ref, grouped_ref, normed_ref, pooled_ref):
    hot = one_hot_rows(pl.program_id(0) * 256, 256, row_ref[...])
    rows = mm(hot, x_ref[...])
    grouped_ref[...] = rows.astype(BF16)
    mean = jnp.mean(rows * rows, axis=-1, keepdims=True)
    normed = (rows * lax.rsqrt(mean + 1e-5) * gain_ref[...]).astype(BF16)
    normed_ref[...] = normed
    r = lax.broadcasted_iota(jnp.int32, (CK, BALL), 0)
    c = lax.broadcasted_iota(jnp.int32, (CK, BALL), 1)
    pool = jnp.where(c // POOL == r, 1.0 / POOL, 0.0).astype(BF16)
    pooled_ref[...] = mm(pool, normed).astype(BF16)


def place(row, x, gain):
    return pl.pallas_call(
        place_kernel,
        grid=(NB,),
        in_specs=[fixed((1, ROWS)), fixed((ROWS, D)), fixed((1, D))],
        out_specs=[
            pl.BlockSpec((BALL, D), lambda i: (i, 0)),
            pl.BlockSpec((BALL, D), lambda i: (i, 0)),
            pl.BlockSpec((CK, D), lambda i: (i, 0)),
        ],
        out_shape=[
            jax.ShapeDtypeStruct((ROWS, D), BF16),
            jax.ShapeDtypeStruct((ROWS, D), BF16),
            jax.ShapeDtypeStruct((NB * CK, D), BF16),
        ],
        compiler_params=pltpu.CompilerParams(vmem_limit_bytes=VMEM_LIMIT),
        name="place",
    )(row, x, gain)


def head_norm_cols(u):
    shaped = u.reshape(HEADS, HD, u.shape[1])
    mean = jnp.mean(shaped * shaped, axis=1, keepdims=True)
    return (shaped * lax.rsqrt(mean + 1e-6)).astype(BF16)


def layer_kernel(
    chosen_ref, normed_ref, grouped_ref, cand_ref, wq_ref, wk_ref, wv_ref, wpk_ref,
    wpv_ref, wo_ref, wg_ref, wu_ref, wd_ref, scale_ref, gain_ref, mix_ref, sum_ref,
    out_ref, keys, values, probs, partial,
):
    ball = pl.program_id(0)

    @pl.when(ball == 0)
    def _():
        keys[...] = jnp.zeros_like(keys)
        values[...] = jnp.zeros_like(values)

    normed = normed_ref[...]
    q = mm(normed, wq_ref[...])
    square = (q * q).astype(BF16)
    mean = jnp.concatenate(
        [mm(square[:, :256], mix_ref[...]), mm(square[:, 256:], mix_ref[...])], axis=1)
    query = (q * lax.rsqrt(mean + 1e-6) * scale_ref[...]).astype(BF16)
    near_key = head_norm_cols(mm_nt(wk_ref[...], normed))
    near_value = mm(normed, wv_ref[...]).astype(BF16)
    picked = jnp.concatenate(
        [cand_ref[pl.ds(pl.multiple_of(chosen_ref[ball, j] * CK, CK), CK), :]
         for j in range(OWNERS)], axis=0)
    far_key = head_norm_cols(mm_nt(wpk_ref[...], picked))
    far_value = mm(picked, wpv_ref[...]).astype(BF16)
    lane = lax.broadcasted_iota(jnp.int32, (1, 128), 1) // HD
    for h in range(HEADS):
        g, l = h // GROUP, h % GROUP
        at = l * KEYS
        r = slice(l * HD, (l + 1) * HD)
        keys[g, r, at:at + BALL] = near_key[h]
        keys[g, r, at + BALL:at + KEYS] = far_key[h]
        t = l // 4
        cols = slice(g * 256 + t * 128, g * 256 + t * 128 + 128)
        mask = lane == (l % 4)
        zero = jnp.zeros((), BF16)
        values[g, at:at + BALL, t * 128:(t + 1) * 128] = jnp.where(
            mask, near_value[:, cols], zero)
        values[g, at + BALL:at + KEYS, t * 128:(t + 1) * 128] = jnp.where(
            mask, far_value[:, cols], zero)
    attended = []
    for g in range(HEADS // GROUP):
        qg = query[:, g * 256:(g + 1) * 256]
        for l in range(GROUP):
            p = jnp.exp2(mm(qg, keys[g, :, l * KEYS:(l + 1) * KEYS]))
            probs[:, l * KEYS:(l + 1) * KEYS] = p.astype(BF16)
            partial[:, l * 128:(l + 1) * 128] = (
                p[:, :128] + p[:, 128:256] + p[:, 256:384]).astype(BF16)
        total = mm(probs[...], values[g])
        denominator = mm(partial[...], sum_ref[...])
        attended.append((total / denominator).astype(BF16))
    attended = jnp.concatenate(attended, axis=1)
    residual = (grouped_ref[...].astype(F32) + mm(attended, wo_ref[...])).astype(BF16)
    wide = residual.astype(F32)
    mean = jnp.mean(wide * wide, axis=-1, keepdims=True)
    ffn = (wide * lax.rsqrt(mean + 1e-5) * gain_ref[...]).astype(BF16)
    gate = mm(ffn, wg_ref[...])
    up = mm(ffn, wu_ref[...])
    hidden = (gate / (1.0 + jnp.exp(-gate)) * up).astype(BF16)
    out_ref[...] = (wide + mm(hidden, wd_ref[...])).astype(BF16)


def layer(chosen, normed, grouped, cand, weights):
    rows = pl.BlockSpec((BALL, D), lambda i, _: (i, 0))
    return pl.pallas_call(
        layer_kernel,
        grid_spec=pltpu.PrefetchScalarGridSpec(
            num_scalar_prefetch=1,
            grid=(NB,),
            in_specs=[rows, rows, fixed(cand.shape)] + [fixed(w.shape) for w in weights],
            out_specs=rows,
            scratch_shapes=[
                pltpu.VMEM((2, 256, GROUP * KEYS), BF16),
                pltpu.VMEM((2, GROUP * KEYS, 256), BF16),
                pltpu.VMEM((BALL, GROUP * KEYS), BF16),
                pltpu.VMEM((BALL, GROUP * 128), BF16),
            ],
        ),
        out_shape=jax.ShapeDtypeStruct((ROWS, D), BF16),
        compiler_params=pltpu.CompilerParams(vmem_limit_bytes=VMEM_LIMIT),
        name="layer",
    )(chosen, normed, grouped, cand, *weights)


def pick_kernel(col_ref, x_ref, out_ref):
    hot = one_hot_cols(col_ref[...], 256)
    out_ref[...] = mm(hot, x_ref[...]).astype(BF16)


def pick(col, x):
    return pl.pallas_call(
        pick_kernel,
        grid=(NB,),
        in_specs=[pl.BlockSpec((256, 1), lambda i: (i, 0)), fixed((ROWS, D))],
        out_specs=pl.BlockSpec((256, D), lambda i: (i, 0)),
        out_shape=jax.ShapeDtypeStruct((ROWS, D), BF16),
        compiler_params=pltpu.CompilerParams(vmem_limit_bytes=VMEM_LIMIT),
        name="pick",
    )(col, x)


def from_behind(block, distance):
    route = [((i - distance) % PEERS, i) for i in range(PEERS)]
    return lax.ppermute(block, "pts", route)


def on_device(
    points, point_row_index, neighbour_ball_list, attention_norm_gain, query_weight,
    key_weight, value_weight, pooled_key_weight, pooled_value_weight, head_score_scale,
    output_weight, feedforward_norm_gain, gate_weight, up_weight, down_weight,
):
    me = lax.axis_index("pts")
    outgoing, ids, pos = pack(
        point_row_index.reshape(ROWS, 1), point_row_index.reshape(1, ROWS), points)
    arrived, all_ids = exchange(outgoing, ids)
    mine = lax.dynamic_slice_in_dim(all_ids.reshape(PEERS, 128), (me % 4) * EACH, EACH, 1)
    slot = mine.reshape(ROWS) - me * ROWS
    grouped, normed, pooled = place(
        slot.reshape(1, ROWS), arrived.reshape(ROWS, D), attention_norm_gain.reshape(1, D))
    blocks = [from_behind(pooled, k) if k else pooled for k in range(REACH, -REACH - 1, -1)]
    cand = jnp.concatenate(blocks, axis=0)
    owner = neighbour_ball_list // NB
    offset = jnp.mod(owner - me + REACH, PEERS)
    chosen = offset * NB + neighbour_ball_list % NB
    scale = jnp.repeat(head_score_scale * (math.log2(math.e) / HD), HD).reshape(1, D)
    a = lax.broadcasted_iota(jnp.int32, (256, 256), 0) // HD
    b = lax.broadcasted_iota(jnp.int32, (256, 256), 1) // HD
    mix = jnp.where(a == b, 1.0 / HD, 0.0).astype(BF16)
    a = lax.broadcasted_iota(jnp.int32, (GROUP * 128, 256), 0) // 128
    b = lax.broadcasted_iota(jnp.int32, (GROUP * 128, 256), 1) // HD
    spread = jnp.where(a == b, 1.0, 0.0).astype(BF16)
    ball_out = layer(
        chosen, normed, grouped, cand,
        (query_weight, key_weight.T, value_weight, pooled_key_weight.T, pooled_value_weight,
         output_weight, gate_weight, up_weight, down_weight, scale,
         feedforward_norm_gain.reshape(1, D), mix, spread))
    returning = pick(slot.reshape(ROWS, 1), ball_out)
    came_back = exchange(returning)
    return pick(pos.reshape(ROWS, 1), came_back.reshape(ROWS, D))


def solution(mesh):
    return jax.shard_map(
        on_device,
        mesh=mesh,
        in_specs=(
            P(("rep", "pts"), None), P(("rep", "pts")), P(("rep", "pts"), None),
            P(), P(), P(), P(), P(), P(), P(), P(), P(), P(), P(), P(),
        ),
        out_specs=P(("rep", "pts"), None),
        check_vma=False,
    )
```

time: 368 us -> 213 us (0.58)
  Pallas kernels: 0 us -> 165 us
  matrix products: 97.1 us -> 0 us
  waiting for transfers between devices: 82.4 us -> 14 us
  local copies, waits for them, and re-layouts: 76 us -> 11.2 us
  other arithmetic: 40.1 us -> 4.55 us
  starting transfers between devices: 50.1 us -> 17.8 us
  loops' own time: 20.1 us -> 0 us
    pallas_call x0 -> x7, Pallas kernels: none -> 165 us  [the longest x2 78.5 us: exchange(): pl.pallas_call(functools.partial(exchange_kernel, with_ids), in_specs=vme...]
    dot_general x39 -> x0, matrix products: 97.1 us -> none  [the longest x8 21.4 us: one_ball(): jnp.einsum('hdq,hde->qe', attended, output_heads, preferred_element_type=...]
    gather x6 -> x0, local copies, waits for them, and re-layouts: 53.7 us -> none  [the longest x1 11.8 us: on_device(): jnp.take(point_row_index, sort_order, axis=0).reshape(peer_count, send_each)]
    all_to_all x3 -> x0, waiting for transfers between devices: 50.7 us -> none  [the longest x1 25.7 us: on_device(): lax.all_to_all(returning, 'pts', split_axis=0, concat_axis=0, tiled=True)]
    all_to_all x3 -> x0, starting transfers between devices: 39.1 us -> none  [the longest x1 16.3 us: on_device(): lax.all_to_all(returning, 'pts', split_axis=0, concat_axis=0, tiled=True)]
    another operation x1 -> x0, loops' own time: 20.1 us -> none  [on_device(): lax.map(one_ball, jnp.arange(blocks_dev, dtype=jnp.int32))]
    ppermute x8, waiting for transfers between devices: 31.7 us -> 14 us  [from_behind(): return lax.ppermute(block, 'pts', route)]
    sort x3 -> x0, other arithmetic: 16 us -> none  [the longest x1 5.89 us: on_device(): sort_order = jnp.argsort(point_row_index)]
  transfers between devices with their start and end apart: 11 -> 8, of which waited for: 8 -> 2; matrix products, arithmetic and copies ran while one was open for 9% -> 4% of each run, Pallas kernels for 0% -> 0%
where the time goes in v1:
time: 213 us; the launch traced here: 212 us
  Pallas kernels  165 us (77%)
  starting transfers between devices  17.8 us (8%)
  waiting for transfers between devices  14 us (7%)
  local copies, waits for them, and re-layouts  11.2 us (5%)
  other arithmetic  4.55 us (2%)
    pallas_call x2, Pallas kernels, exchange(): pl.pallas_call(functools.partial(exchange_kernel, with_ids), in_specs=vme...  78.5 us
    pallas_call x1, Pallas kernels, layer(): pl.pallas_call(layer_kernel, grid_spec=pltpu.PrefetchScalarGridSpec(num_s...  45.7 us
    pallas_call x2, Pallas kernels, pick(): pl.pallas_call(pick_kernel, grid=(NB,), in_specs=[pl.BlockSpec((256, 1),...  18.4 us
    ppermute x8, starting transfers between devices, from_behind(): return lax.ppermute(block, 'pts', route)  17.8 us
    ppermute x8, waiting for transfers between devices, from_behind(): return lax.ppermute(block, 'pts', route)  14 us
    pallas_call x1, Pallas kernels, pack(): pl.pallas_call(pack_kernel, grid=(NB,), in_specs=[fixed((ROWS, 1)), fixed...  12.5 us
    pallas_call x1, Pallas kernels, place(): pl.pallas_call(place_kernel, grid=(NB,), in_specs=[fixed((1, ROWS)), fixe...  9.65 us
  transfers between devices with their start and end apart: 8, of which 2 were waited for; matrix products, arithmetic and copies ran while one was open for 4% of the time, Pallas kernels for 0%

profile of v1, /device:TPU:1, one launch (start us, length us, event | category | flops | bytes accessed | tf_op | source)
XLA Modules:
  0.0 212.4 jit_solution(6213704444079132759)
XLA Ops:
  0.0 2.0 copy.22.col_ref
  2.0 12.5 %pack.1 = (bf16[2048,512]{1,0:T(8,128)(2,1)}, s32[16,1,128]{2,1,0:T(1,128)}, s32[1,2048]{1,0:T(1,128)}) custom-call(s32[2048,1]{1,0:T(8,128)} %copy.22.col_ref, s32[1,2048]{1,0:T(1,128)} %bitcast.20, bf16[2048,512]{1,0:T(8,128)(2,1)} %x_ref.1), custom_call_target="tpu_custom_call" | custom-call | tf_op jit(solution)/shard_map/pack/pallas_call | solution.py:87
  14.5 41.2 %exchange_ids.1 = (bf16[64,32,512]{2,1,0:T(8,128)(2,1)}, s32[64,1,128]{2,1,0:T(1,128)}) custom-call(bf16[64,32,512]{2,1,0:T(8,128)(2,1)} %bitcast.17, s32[16,1,128]{2,1,0:T(1,128)} %get-tuple-element.15.refs_1_), custom_call_target="tpu_custom_call" | custom-call | tf_op jit(solution)/shard_map/exchange_ids/pallas_call | solution.py:179
  56.3 1.6 fusion.9
  57.9 0.7 sub.66.row_ref
  58.5 9.7 %place.1 = (bf16[2048,512]{1,0:T(8,128)(2,1)}, bf16[2048,512]{1,0:T(8,128)(2,1)}, bf16[256,512]{1,0:T(8,128)(2,1)}) custom-call(s32[1,2048]{1,0:T(1,128)} %sub.66.row_ref, bf16[2048,512]{1,0:T(8,128)(2,1)} %bitcast.16, f32[1,512]{1,0:T(1,128)} %bitcast.22), custom_call_target="tpu_custom_call" | custom-call | tf_op jit(solution)/shard_map/place/pallas_call | solution.py:205
  68.2 1.3 collective-permute-start
  69.5 5.6 %collective-permute-start.1 = (bf16[256,512]{1,0:T(8,128)(2,1)}, bf16[256,512]{1,0:T(8,128)(2,1)S(1)}, u32[]{:S(2)}, u32[]{:S(2)}) collective-permute-start(bf16[256,512]{1,0:T(8,128)(2,1)} %get-tuple-element.20), channel_id=1, source_target_pairs={{122,0},{124,2},{126,4},{0,6},{2,8},{4,10},{6,12},{8,14},{10,16},{... | collective-permute-start | bytes 786440 | tf_op jit(solution)/shard_map/ppermute | solution.py:333
  75.7 0.8 select_convert_fusion.1.mix_ref
  76.6 1.5 select_convert_fusion.sum_ref
  78.7 1.1 copy.27
  79.7 1.0 copy.28
  80.8 0.6 reshape_reshape.3.scale_ref
  81.4 2.2 %sub.69.col_ref = s32[2048,1]{1,0:T(8,128)} reshape(s32[64,32]{1,0:T(8,128)S(1)} %get-tuple-element.21) | data formatting | bytes 16384 | tf_op jit(solution)/shard_map/sub | solution.py:346
  83.6 1.3 copy.30.col_ref
  84.9 7.2 %collective-permute-start.5 = (bf16[256,512]{1,0:T(8,128)(2,1)S(1)}, bf16[256,512]{1,0:T(8,128)(2,1)S(1)}, u32[]{:S(2)}, u32[]{:S(2)}) collective-permute-start(bf16[256,512]{1,0:T(8,128)(2,1)S(1)} %copy-done.3), channel_id=1, source_target_pairs={{4,0},{6,2},{8,4},{10,6},{12,8},{14,10},{16,12},{18,14},{20,16},{2... | collective-permute-start | bytes 786440 | tf_op jit(solution)/shard_map/ppermute | solution.py:333
  92.3 3.1 %collective-permute-start.7 = (bf16[256,512]{1,0:T(8,128)(2,1)S(1)}, bf16[256,512]{1,0:T(8,128)(2,1)S(1)}, u32[]{:S(2)}, u32[]{:S(2)}) collective-permute-start(bf16[256,512]{1,0:T(8,128)(2,1)S(1)} %copy-done.3), channel_id=1, source_target_pairs={{8,0},{10,2},{12,4},{14,6},{16,8},{18,10},{20,12},{22,14},{24,16},... | collective-permute-start | bytes 786440 | tf_op jit(solution)/shard_map/ppermute | solution.py:333
  95.5 2.3 %collective-permute-done.5 = bf16[256,512]{1,0:T(8,128)(2,1)S(1)} collective-permute-done((bf16[256,512]{1,0:T(8,128)(2,1)S(1)}, bf16[256,512]{1,0:T(8,128)(2,1)S(1)}, u32[]{:S(2)}, u32[]{:S(2)}) %collective-permute-start.5) | collective-permute-done | bytes 262176 | tf_op jit(solution)/shard_map/ppermute | solution.py:333
  97.8 11.7 %collective-permute-done.6 = bf16[256,512]{1,0:T(8,128)(2,1)S(1)} collective-permute-done((bf16[256,512]{1,0:T(8,128)(2,1)S(1)}, bf16[256,512]{1,0:T(8,128)(2,1)S(1)}, u32[]{:S(2)}, u32[]{:S(2)}) %collective-permute-start.6) | collective-permute-done | bytes 262176 | tf_op jit(solution)/shard_map/ppermute | solution.py:333
  109.6 1.4 copy-done
  111.0 45.7 %layer.1.x_ref = bf16[2048,512]{1,0:T(8,128)(2,1)} custom-call(s32[8,4]{1,0:T(8,128)} %fusion.4.chosen_ref, bf16[2048,512]{1,0:T(8,128)(2,1)} %get-tuple-element.18.normed_ref, bf16[2048,512]{1,0:T(8,128)(2,1)} %get-tuple-element.19.grouped_ref, bf16[2304,512]{1,0:T(8,128)(2,1)} %copy-done, bf16[512,512]{1,0:T(8,128)(2,1)} %wq_ref.1, ...), custom_call_target="tpu_custom_call" | custom-call | tf_op jit(solution)/shard_map/layer/pallas_call | solution.py:294
  156.7 9.2 %pick.2 = bf16[2048,512]{1,0:T(8,128)(2,1)} custom-call(s32[2048,1]{1,0:T(8,128)} %sub.69.col_ref, bf16[2048,512]{1,0:T(8,128)(2,1)} %layer.1.x_ref), custom_call_target="tpu_custom_call" | custom-call | tf_op jit(solution)/shard_map/pick/pallas_call | solution.py:320
  165.9 37.3 %exchange.1 = bf16[64,32,512]{2,1,0:T(8,128)(2,1)} custom-call(bf16[64,32,512]{2,1,0:T(8,128)(2,1)} %bitcast.12), custom_call_target="tpu_custom_call" | custom-call | tf_op jit(solution)/shard_map/exchange/pallas_call | solution.py:179
  203.2 9.2 %pick.3 = bf16[2048,512]{1,0:T(8,128)(2,1)} custom-call(s32[2048,1]{1,0:T(8,128)} %copy.30.col_ref, bf16[2048,512]{1,0:T(8,128)(2,1)} %bitcast.13), custom_call_target="tpu_custom_call" | custom-call | tf_op jit(solution)/shard_map/pick/pallas_call | solution.py:320
  (41 shorter events, 2.1 us)
Async XLA Ops:
  14.5 61.1 %copy-start.5 = (s32[8,4]{0,1:T(4,128)S(1)}, s32[8,4]{0,1:T(4,128)}, u32[]{:S(2)}) copy-start(s32[8,4]{0,1:T(4,128)} %param.17) | copy-start | bytes 388
  14.5 64.2 %copy-start.6 = (f32[16]{0:T(128)S(1)}, f32[16]{0:T(128)}, u32[]{:S(2)}) copy-start(f32[16]{0:T(128)} %param.24) | copy-start | bytes 196
  14.5 64.2 %copy-start.1 = (bf16[512,512]{1,0:T(8,128)(2,1)S(1)}, bf16[512,512]{1,0:T(8,128)(2,1)}, u32[]{:S(2)}) copy-start(bf16[512,512]{1,0:T(8,128)(2,1)} %param.20) | copy-start | bytes 1572868
  55.8 24.0 %copy-start.2 = (bf16[512,512]{1,0:T(8,128)(2,1)S(1)}, bf16[512,512]{1,0:T(8,128)(2,1)}, u32[]{:S(2)}) copy-start(bf16[512,512]{1,0:T(8,128)(2,1)} %param.22) | copy-start | bytes 1572868
  68.2 15.4 %copy-start.4 = (s32[1,2048]{1,0:T(1,128)S(1)}, s32[1,2048]{1,0:T(1,128)}, u32[]{:S(2)}) copy-start(s32[1,2048]{1,0:T(1,128)} %get-tuple-element.13) | copy-start | bytes 24580
  68.2 16.7 %collective-permute-start = (bf16[256,512]{1,0:T(8,128)(2,1)}, bf16[256,512]{1,0:T(8,128)(2,1)S(1)}, u32[]{:S(2)}, u32[]{:S(2)}) collective-permute-start(bf16[256,512]{1,0:T(8,128)(2,1)} %get-tuple-element.20), channel_id=1, source_target_pairs={{120,0},{122,2},{124,4},{126,6},{0,8},{2,10},{4,12},{6,14},{8,16},... | collective-permute-start | bytes 786440 | tf_op jit(solution)/shard_map/ppermute | solution.py:333
  69.5 22.6 %collective-permute-start.1 = (bf16[256,512]{1,0:T(8,128)(2,1)}, bf16[256,512]{1,0:T(8,128)(2,1)S(1)}, u32[]{:S(2)}, u32[]{:S(2)}) collective-permute-start(bf16[256,512]{1,0:T(8,128)(2,1)} %get-tuple-element.20), channel_id=1, source_target_pairs={{122,0},{124,2},{126,4},{0,6},{2,8},{4,10},{6,12},{8,14},{10,16},{... | collective-permute-start | bytes 786440 | tf_op jit(solution)/shard_map/ppermute | solution.py:333
  75.1 17.2 %collective-permute-start.2 = (bf16[256,512]{1,0:T(8,128)(2,1)}, bf16[256,512]{1,0:T(8,128)(2,1)S(1)}, u32[]{:S(2)}, u32[]{:S(2)}) collective-permute-start(bf16[256,512]{1,0:T(8,128)(2,1)} %get-tuple-element.20), channel_id=1, source_target_pairs={{124,0},{126,2},{0,4},{2,6},{4,8},{6,10},{8,12},{10,14},{12,16},{1... | collective-permute-start | bytes 786440 | tf_op jit(solution)/shard_map/ppermute | solution.py:333
  75.1 20.3 %collective-permute-start.3 = (bf16[256,512]{1,0:T(8,128)(2,1)}, bf16[256,512]{1,0:T(8,128)(2,1)S(1)}, u32[]{:S(2)}, u32[]{:S(2)}) collective-permute-start(bf16[256,512]{1,0:T(8,128)(2,1)} %get-tuple-element.20), channel_id=1, source_target_pairs={{126,0},{0,2},{2,4},{4,6},{6,8},{8,10},{10,12},{12,14},{14,16},{16... | collective-permute-start | bytes 786440 | tf_op jit(solution)/shard_map/ppermute | solution.py:333
  75.2 20.3 %collective-permute-start.4 = (bf16[256,512]{1,0:T(8,128)(2,1)}, bf16[256,512]{1,0:T(8,128)(2,1)S(1)}, u32[]{:S(2)}, u32[]{:S(2)}) collective-permute-start(bf16[256,512]{1,0:T(8,128)(2,1)} %get-tuple-element.20), channel_id=1, source_target_pairs={{2,0},{4,2},{6,4},{8,6},{10,8},{12,10},{14,12},{16,14},{18,16},{20... | collective-permute-start | bytes 786440 | tf_op jit(solution)/shard_map/ppermute | solution.py:333
  76.6 8.4 %copy-start.3 = (bf16[256,512]{1,0:T(8,128)(2,1)S(1)}, bf16[256,512]{1,0:T(8,128)(2,1)}, u32[]{:S(2)}) copy-start(bf16[256,512]{1,0:T(8,128)(2,1)} %get-tuple-element.20) | copy-start | bytes 786436
  84.9 12.8 %collective-permute-start.5 = (bf16[256,512]{1,0:T(8,128)(2,1)S(1)}, bf16[256,512]{1,0:T(8,128)(2,1)S(1)}, u32[]{:S(2)}, u32[]{:S(2)}) collective-permute-start(bf16[256,512]{1,0:T(8,128)(2,1)S(1)} %copy-done.3), channel_id=1, source_target_pairs={{4,0},{6,2},{8,4},{10,6},{12,8},{14,10},{16,12},{18,14},{20,16},{2... | collective-permute-start | bytes 786440 | tf_op jit(solution)/shard_map/ppermute | solution.py:333
  92.2 17.3 %collective-permute-start.6 = (bf16[256,512]{1,0:T(8,128)(2,1)S(1)}, bf16[256,512]{1,0:T(8,128)(2,1)S(1)}, u32[]{:S(2)}, u32[]{:S(2)}) collective-permute-start(bf16[256,512]{1,0:T(8,128)(2,1)S(1)} %copy-done.3), channel_id=1, source_target_pairs={{6,0},{8,2},{10,4},{12,6},{14,8},{16,10},{18,12},{20,14},{22,16},{... | collective-permute-start | bytes 786440 | tf_op jit(solution)/shard_map/ppermute | solution.py:333
  92.3 17.2 %collective-permute-start.7 = (bf16[256,512]{1,0:T(8,128)(2,1)S(1)}, bf16[256,512]{1,0:T(8,128)(2,1)S(1)}, u32[]{:S(2)}, u32[]{:S(2)}) collective-permute-start(bf16[256,512]{1,0:T(8,128)(2,1)S(1)} %copy-done.3), channel_id=1, source_target_pairs={{8,0},{10,2},{12,4},{14,6},{16,8},{18,10},{20,12},{22,14},{24,16},... | collective-permute-start | bytes 786440 | tf_op jit(solution)/shard_map/ppermute | solution.py:333
  109.5 1.4 copy-start

commit v2 on v1

--- a/solution.py
+++ b/solution.py
@@ -11,7 +11,6 @@
 BALL = 256
 POOL = 8
 OWNERS = 4
-REACH = 4
 D = 512
 HEADS = 16
 HD = 32
@@ -23,6 +22,7 @@
 KEYS = BALL + OWNERS * CK
 GROUP = 8
 NB = ROWS // BALL
+CHIPS = PEERS // 2
 MESH = pl.DeviceIdType.MESH
 F32 = jnp.float32
 BF16 = jnp.bfloat16
@@ -227,88 +227,234 @@
     return (shaped * lax.rsqrt(mean + 1e-6)).astype(BF16)
 
 
-def layer_kernel(
-    chosen_ref, normed_ref, grouped_ref, cand_ref, wq_ref, wk_ref, wv_ref, wpk_ref,
-    wpv_ref, wo_ref, wg_ref, wu_ref, wd_ref, scale_ref, gain_ref, mix_ref, sum_ref,
-    out_ref, keys, values, probs, partial,
-):
-    ball = pl.program_id(0)
-
-    @pl.when(ball == 0)
-    def _():
-        keys[...] = jnp.zeros_like(keys)
-        values[...] = jnp.zeros_like(values)
-
-    normed = normed_ref[...]
-    q = mm(normed, wq_ref[...])
-    square = (q * q).astype(BF16)
-    mean = jnp.concatenate(
-        [mm(square[:, :256], mix_ref[...]), mm(square[:, 256:], mix_ref[...])], axis=1)
-    query = (q * lax.rsqrt(mean + 1e-6) * scale_ref[...]).astype(BF16)
-    near_key = head_norm_cols(mm_nt(wk_ref[...], normed))
-    near_value = mm(normed, wv_ref[...]).astype(BF16)
-    picked = jnp.concatenate(
-        [cand_ref[pl.ds(pl.multiple_of(chosen_ref[ball, j] * CK, CK), CK), :]
-         for j in range(OWNERS)], axis=0)
-    far_key = head_norm_cols(mm_nt(wpk_ref[...], picked))
-    far_value = mm(picked, wpv_ref[...]).astype(BF16)
+def block_ones(rows, per_row, per_col, value):
+    a = lax.broadcasted_iota(jnp.int32, (rows, 256), 0) // per_row
+    b = lax.broadcasted_iota(jnp.int32, (rows, 256), 1) // per_col
+    return jnp.where(a == b, value, 0.0).astype(BF16)
+
+
+def set_heads(keys, values, key, value, count):
     lane = lax.broadcasted_iota(jnp.int32, (1, 128), 1) // HD
+    zero = jnp.zeros((), BF16)
     for h in range(HEADS):
         g, l = h // GROUP, h % GROUP
-        at = l * KEYS
-        r = slice(l * HD, (l + 1) * HD)
-        keys[g, r, at:at + BALL] = near_key[h]
-        keys[g, r, at + BALL:at + KEYS] = far_key[h]
         t = l // 4
+        at = slice(l * count, (l + 1) * count)
+        keys[g, l * HD:(l + 1) * HD, at] = key[h]
         cols = slice(g * 256 + t * 128, g * 256 + t * 128 + 128)
-        mask = lane == (l % 4)
-        zero = jnp.zeros((), BF16)
-        values[g, at:at + BALL, t * 128:(t + 1) * 128] = jnp.where(
-            mask, near_value[:, cols], zero)
-        values[g, at + BALL:at + KEYS, t * 128:(t + 1) * 128] = jnp.where(
-            mask, far_value[:, cols], zero)
-    attended = []
-    for g in range(HEADS // GROUP):
-        qg = query[:, g * 256:(g + 1) * 256]
-        for l in range(GROUP):
-            p = jnp.exp2(mm(qg, keys[g, :, l * KEYS:(l + 1) * KEYS]))
-            probs[:, l * KEYS:(l + 1) * KEYS] = p.astype(BF16)
-            partial[:, l * 128:(l + 1) * 128] = (
-                p[:, :128] + p[:, 128:256] + p[:, 256:384]).astype(BF16)
-        total = mm(probs[...], values[g])
-        denominator = mm(partial[...], sum_ref[...])
-        attended.append((total / denominator).astype(BF16))
-    attended = jnp.concatenate(attended, axis=1)
-    residual = (grouped_ref[...].astype(F32) + mm(attended, wo_ref[...])).astype(BF16)
-    wide = residual.astype(F32)
-    mean = jnp.mean(wide * wide, axis=-1, keepdims=True)
-    ffn = (wide * lax.rsqrt(mean + 1e-5) * gain_ref[...]).astype(BF16)
-    gate = mm(ffn, wg_ref[...])
-    up = mm(ffn, wu_ref[...])
-    hidden = (gate / (1.0 + jnp.exp(-gate)) * up).astype(BF16)
-    out_ref[...] = (wide + mm(hidden, wd_ref[...])).astype(BF16)
-
-
-def layer(chosen, normed, grouped, cand, weights):
-    rows = pl.BlockSpec((BALL, D), lambda i, _: (i, 0))
+        values[g, at, t * 128:(t + 1) * 128] = jnp.where(lane == (l % 4), value[:, cols], zero)
+
+
+def attention_kernel(
+    chosen_ref, normed_ref, grouped_ref, pooled_ref, wq_ref, wk_ref, wv_ref, wpk_ref,
+    wpv_ref, wo_ref, scale_ref, out_ref,
+    cand, near_keys, near_values, far_keys, far_values, probs, partial, queries,
+    totals, sums, wk_t, wpk_t, mix, spread, send, recv, here,
+):
+    me = lax.axis_index("pts")
+    core = me % 2
+    chip = me // 2
+    partner = chip * 2 + 1 - core
+    steps = (1, -1, 2, -2)
+
+    def chip_at(e):
+        return ((chip + e + CHIPS) % CHIPS) * 2 + core
+
+    barrier = pltpu.get_barrier_semaphore()
+    for d in [partner] + [chip_at(e) for e in steps]:
+        pl.semaphore_signal(barrier, inc=1, device_id={"pts": d}, device_id_type=MESH)
+    pl.semaphore_wait(barrier, 1 + len(steps))
+
+    def block(slot):
+        return cand.at[pl.ds(slot * NB, NB)]
+
+    def remote(src, slot, at, d):
+        return pltpu.make_async_remote_copy(
+            src_ref=src, dst_ref=block(slot), send_sem=send.at[at], recv_sem=recv.at[at],
+            device_id={"pts": d}, device_id_type=MESH)
+
+    outs = [remote(pooled_ref, (2 - e) * 2 + core, 1 + i, chip_at(e))
+            for i, e in enumerate(steps)]
+    for copy in outs:
+        copy.start()
+    to_partner = remote(pooled_ref, 4 + core, 0, partner)
+    to_partner.start()
+    own = pltpu.make_async_copy(pooled_ref, block(4 + core), here.at[0])
+    own.start()
+    onward = [remote(block((2 - e) * 2 + core), (2 - e) * 2 + core, 5 + i, partner)
+              for i, e in enumerate(steps)]
+
+    for ref in (near_keys, near_values, far_keys, far_values):
+        ref[...] = jnp.zeros_like(ref)
+    wk_t[...] = wk_ref[...].T
+    wpk_t[...] = wpk_ref[...].T
+    mix[...] = block_ones(256, HD, HD, 1.0 / HD)
+    spread[...] = block_ones(GROUP * 128, 128, HD, 1.0)
+
+    def near(ball, carry):
+        for at, pair in ((5, (0, 1)), (7, (2, 3))):
+            @pl.when(ball == at)
+            def _():
+                for i in pair:
+                    outs[i].wait_recv()
+                    onward[i].start()
+
+        rows = pl.ds(pl.multiple_of(ball * BALL, BALL), BALL)
+        normed = normed_ref[rows, :]
+        q = mm(normed, wq_ref[...])
+        square = (q * q).astype(BF16)
+        mean = jnp.concatenate(
+            [mm(square[:, :256], mix[...]), mm(square[:, 256:], mix[...])], axis=1)
+        query = (q * lax.rsqrt(mean + 1e-6) * scale_ref[...]).astype(BF16)
+        queries[rows, :] = query
+        key = head_norm_cols(mm_nt(wk_t[...], normed))
+        value = mm(normed, wv_ref[...]).astype(BF16)
+        set_heads(near_keys, near_values, key, value, BALL)
+        for g in range(HEADS // GROUP):
+            cols = slice(g * 256, (g + 1) * 256)
+            qg = query[:, cols]
+            for l in range(GROUP):
+                p = jnp.exp2(mm(qg, near_keys[g, :, l * BALL:(l + 1) * BALL]))
+                probs[:, l * BALL:(l + 1) * BALL] = p.astype(BF16)
+                partial[:, l * 128:(l + 1) * 128] = (p[:, :128] + p[:, 128:]).astype(BF16)
+            totals[rows, cols] = mm(probs[...], near_values[g])
+            sums[rows, cols] = mm(partial[...], spread[...])
+        return carry
+
+    lax.fori_loop(0, NB, near, 0)
+    own.wait()
+    to_partner.wait()
+    for copy in outs:
+        copy.wait_send()
+    for copy in onward:
+        copy.wait()
+
+    def far(ball, carry):
+        rows = pl.ds(pl.multiple_of(ball * BALL, BALL), BALL)
+        picked = []
+        for j in range(OWNERS):
+            picked.append(cand[chosen_ref[ball, j]])
+        picked = jnp.concatenate(picked, axis=0)
+        key = head_norm_cols(mm_nt(wpk_t[...], picked))
+        value = mm(picked, wpv_ref[...]).astype(BF16)
+        set_heads(far_keys, far_values, key, value, OWNERS * CK)
+        attended = []
+        for g in range(HEADS // GROUP):
+            cols = slice(g * 256, (g + 1) * 256)
+            qg = queries[rows, cols]
+            for l in range(GROUP // 2):
+                p = jnp.exp2(mm(qg, far_keys[g, :, l * 256:(l + 1) * 256]))
+                partial[:, l * 256:(l + 1) * 256] = p.astype(BF16)
+            total = totals[rows, cols] + mm(partial[...], far_values[g])
+            denominator = sums[rows, cols] + mm(partial[...], spread[...])
+            attended.append((total / denominator).astype(BF16))
+        attended = jnp.concatenate(attended, axis=1)
+        out_ref[rows, :] = (
+            grouped_ref[rows, :].astype(F32) + mm(attended, wo_ref[...])).astype(BF16)
+        return carry
+
+    lax.fori_loop(0, NB, far, 0)
+
+
+def attention(chosen, arrays):
     return pl.pallas_call(
-        layer_kernel,
-        grid_spec=pltpu.PrefetchScalarGridSpec(
-            num_scalar_prefetch=1,
-            grid=(NB,),
-            in_specs=[rows, rows, fixed(cand.shape)] + [fixed(w.shape) for w in weights],
-            out_specs=rows,
-            scratch_shapes=[
-                pltpu.VMEM((2, 256, GROUP * KEYS), BF16),
-                pltpu.VMEM((2, GROUP * KEYS, 256), BF16),
-                pltpu.VMEM((BALL, GROUP * KEYS), BF16),
-                pltpu.VMEM((BALL, GROUP * 128), BF16),
-            ],
-        ),
+        attention_kernel,
+        in_specs=[pl.BlockSpec(memory_space=pltpu.SMEM)] + vmem(len(arrays)),
+        out_specs=vmem(1)[0],
         out_shape=jax.ShapeDtypeStruct((ROWS, D), BF16),
-        compiler_params=pltpu.CompilerParams(vmem_limit_bytes=VMEM_LIMIT),
-        name="layer",
-    )(chosen, normed, grouped, cand, *weights)
+        scratch_shapes=[
+            pltpu.VMEM((10 * NB, CK, D), BF16),
+            pltpu.VMEM((2, 256, GROUP * BALL), BF16),
+            pltpu.VMEM((2, GROUP * BALL, 256), BF16),
+            pltpu.VMEM((2, 256, GROUP * 128), BF16),
+            pltpu.VMEM((2, GROUP * 128, 256), BF16),
+            pltpu.VMEM((BALL, GROUP * BALL), BF16),
+            pltpu.VMEM((BALL, GROUP * 128), BF16),
+            pltpu.VMEM((ROWS, D), BF16),
+            pltpu.VMEM((ROWS, D), F32),
+            pltpu.VMEM((ROWS, D), F32),
+            pltpu.VMEM((D, D), BF16),
+            pltpu.VMEM((D, D), BF16),
+            pltpu.VMEM((256, 256), BF16),
+            pltpu.VMEM((GROUP * 128, 256), BF16),
+            pltpu.SemaphoreType.DMA((9,)),
+            pltpu.SemaphoreType.DMA((9,)),
+            pltpu.SemaphoreType.DMA((1,)),
+        ],
+        compiler_params=pltpu.CompilerParams(
+            collective_id=2, has_side_effects=True, vmem_limit_bytes=VMEM_LIMIT),
+        name="attention",
+    )(chosen, *arrays)
+
+
+def finish_kernel(col_ref, res_ref, wg_ref, wu_ref, wd_ref, gain_ref, out_ref,
+                  ready, send, recv, here):
+    me = lax.axis_index("pts")
+    greet()
+
+    def back(k):
+        d = peer((k * 13) % PEERS)
+        return pltpu.make_async_remote_copy(
+            src_ref=ready.at[k], dst_ref=out_ref.at[me], send_sem=send.at[k],
+            recv_sem=recv.at[k], device_id={"pts": d}, device_id_type=MESH)
+
+    own = pltpu.make_async_copy(ready.at[0], out_ref.at[me], here.at[0])
+
+    def start(k, carry):
+        @pl.when(k > 0)
+        def _():
+            back(k).start()
+
+        @pl.when(k == 0)
+        def _():
+            own.start()
+        return carry
+
+    def chunk(c, carry):
+        cols = [col_ref[pl.ds(pl.multiple_of(peer(((c * 8 + j) * 13) % PEERS) * EACH, EACH),
+                              EACH), :] for j in range(8)]
+        hot = one_hot_cols(jnp.concatenate(cols, axis=0), 256)
+        wide = mm(hot, res_ref[...])
+        mean = jnp.mean(wide * wide, axis=-1, keepdims=True)
+        ffn = (wide * lax.rsqrt(mean + 1e-5) * gain_ref[...]).astype(BF16)
+        gate = mm(ffn, wg_ref[...])
+        up = mm(ffn, wu_ref[...])
+        hidden = (gate / (1.0 + jnp.exp(-gate)) * up).astype(BF16)
+        result = (wide + mm(hidden, wd_ref[...])).astype(BF16)
+        ready[pl.ds(pl.multiple_of(c * 8, 8), 8)] = result.reshape(8, EACH, D)
+
+        @pl.when(c > 0)
+        def _():
+            lax.fori_loop(c * 8 - 8, c * 8, start, 0)
+        return carry
+
+    lax.fori_loop(0, NB, chunk, 0)
+    lax.fori_loop(PEERS - 8, PEERS, start, 0)
+
+    def wait(k, carry):
+        back(k).wait()
+        return carry
+
+    own.wait()
+    lax.fori_loop(1, PEERS, wait, 0)
+
+
+def finish(*arrays):
+    return pl.pallas_call(
+        finish_kernel,
+        in_specs=vmem(len(arrays)),
+        out_specs=vmem(1)[0],
+        out_shape=jax.ShapeDtypeStruct((PEERS, EACH, D), BF16),
+        scratch_shapes=[
+            pltpu.VMEM((PEERS, EACH, D), BF16),
+            pltpu.SemaphoreType.DMA((PEERS,)),
+            pltpu.SemaphoreType.DMA((PEERS,)),
+            pltpu.SemaphoreType.DMA((1,)),
+        ],
+        compiler_params=pltpu.CompilerParams(
+            collective_id=1, has_side_effects=True, vmem_limit_bytes=VMEM_LIMIT),
+        name="finish",
+    )(*arrays)
 
 
 def pick_kernel(col_ref, x_ref, out_ref):
@@ -326,11 +472,6 @@
         compiler_params=pltpu.CompilerParams(vmem_limit_bytes=VMEM_LIMIT),
         name="pick",
     )(col, x)
-
-
-def from_behind(block, distance):
-    route = [((i - distance) % PEERS, i) for i in range(PEERS)]
-    return lax.ppermute(block, "pts", route)
 
 
 def on_device(
@@ -346,25 +487,16 @@
     slot = mine.reshape(ROWS) - me * ROWS
     grouped, normed, pooled = place(
         slot.reshape(1, ROWS), arrived.reshape(ROWS, D), attention_norm_gain.reshape(1, D))
-    blocks = [from_behind(pooled, k) if k else pooled for k in range(REACH, -REACH - 1, -1)]
-    cand = jnp.concatenate(blocks, axis=0)
     owner = neighbour_ball_list // NB
-    offset = jnp.mod(owner - me + REACH, PEERS)
-    chosen = offset * NB + neighbour_ball_list % NB
+    place_of = jnp.mod(owner // 2 - me // 2 + 2, CHIPS) * 2 + owner % 2
+    chosen = place_of * NB + neighbour_ball_list % NB
     scale = jnp.repeat(head_score_scale * (math.log2(math.e) / HD), HD).reshape(1, D)
-    a = lax.broadcasted_iota(jnp.int32, (256, 256), 0) // HD
-    b = lax.broadcasted_iota(jnp.int32, (256, 256), 1) // HD
-    mix = jnp.where(a == b, 1.0 / HD, 0.0).astype(BF16)
-    a = lax.broadcasted_iota(jnp.int32, (GROUP * 128, 256), 0) // 128
-    b = lax.broadcasted_iota(jnp.int32, (GROUP * 128, 256), 1) // HD
-    spread = jnp.where(a == b, 1.0, 0.0).astype(BF16)
-    ball_out = layer(
-        chosen, normed, grouped, cand,
-        (query_weight, key_weight.T, value_weight, pooled_key_weight.T, pooled_value_weight,
-         output_weight, gate_weight, up_weight, down_weight, scale,
-         feedforward_norm_gain.reshape(1, D), mix, spread))
-    returning = pick(slot.reshape(ROWS, 1), ball_out)
-    came_back = exchange(returning)
+    residual = attention(
+        chosen,
+        (normed, grouped, pooled.reshape(NB, CK, D), query_weight, key_weight, value_weight, pooled_key_weight,
+         pooled_value_weight, output_weight, scale))
+    came_back = finish(slot.reshape(ROWS, 1), residual, gate_weight, up_weight, down_weight,
+                       feedforward_norm_gain.reshape(1, D))
     return pick(pos.reshape(ROWS, 1), came_back.reshape(ROWS, D))
 
 

time: 213 us -> 170 us (0.80); the launches traced: 212 us -> 167 us
  starting transfers between devices: 17.8 us -> 0 us
  waiting for transfers between devices: 14 us -> 0 us
  Pallas kernels: 165 us -> 157 us
  local copies, waits for them, and re-layouts: 11.2 us -> 7.48 us
  other arithmetic: 4.55 us -> 2.19 us
    pallas_call x1 -> x2, Pallas kernels: 45.7 us -> 84.8 us  [the longest x1 42.7 us: attention(): pl.pallas_call(attention_kernel, in_specs=[pl.BlockSpec(memory_space=pltp...]
    pallas_call x2 -> x1, Pallas kernels: 78.5 us -> 41.2 us  [exchange(): pl.pallas_call(functools.partial(exchange_kernel, with_ids), in_specs=vme...]
    ppermute x8 -> x0, starting transfers between devices: 17.8 us -> none  [from_behind(): return lax.ppermute(block, 'pts', route)]
    ppermute x8 -> x0, waiting for transfers between devices: 14 us -> none  [from_behind(): return lax.ppermute(block, 'pts', route)]
    pallas_call x2 -> x1, Pallas kernels: 18.4 us -> 9.18 us  [pick(): pl.pallas_call(pick_kernel, grid=(NB,), in_specs=[pl.BlockSpec((256, 1),...]
    unnamed x25 -> x7, local copies, waits for them, and re-layouts: 3.75 us -> 0.09 us
    convert_element_type x2 -> x0, other arithmetic: 2.36 us -> none  [the longest x1 1.52 us: on_device(): spread = jnp.where(a == b, 1.0, 0.0).astype(BF16)]
  transfers between devices with their start and end apart: 8 -> 0, of which waited for: 2 -> 0; matrix products, arithmetic and copies ran while one was open for 4% -> 0% of each run, Pallas kernels for 0% -> 0%
where the time goes in v2:
time: 170 us; the launch traced here: 167 us
  Pallas kernels  157 us (92%)
  local copies, waits for them, and re-layouts  7.48 us (4%)
  other arithmetic  2.19 us (1%)
    pallas_call x1, Pallas kernels, attention(): pl.pallas_call(attention_kernel, in_specs=[pl.BlockSpec(memory_space=pltp...  42.7 us
    pallas_call x1, Pallas kernels, finish(): pl.pallas_call(finish_kernel, in_specs=vmem(len(arrays)), out_specs=vmem(...  42.1 us
    pallas_call x1, Pallas kernels, exchange(): pl.pallas_call(functools.partial(exchange_kernel, with_ids), in_specs=vme...  41.2 us
    pallas_call x1, Pallas kernels, pack(): pl.pallas_call(pack_kernel, grid=(NB,), in_specs=[fixed((ROWS, 1)), fixed...  12.5 us
    pallas_call x1, Pallas kernels, place(): pl.pallas_call(place_kernel, grid=(NB,), in_specs=[fixed((1, ROWS)), fixe...  9.66 us
    pallas_call x1, Pallas kernels, pick(): pl.pallas_call(pick_kernel, grid=(NB,), in_specs=[pl.BlockSpec((256, 1),...  9.18 us

profile of v2, /device:TPU:1, one launch (start us, length us, event | category | flops | bytes accessed | tf_op | source)
XLA Modules:
  0.0 167.0 jit_solution(16140295457362608515)
XLA Ops:
  0.0 2.0 %copy.20.col_ref = s32[2048,1]{1,0:T(8,128)} copy(s32[2048,1]{0,1:T(1,128)} %bitcast.15) | data formatting | bytes 16384 | tf_op jit(solution)/shard_map/reshape | solution.py:484
  2.0 12.5 %pack.1 = (bf16[2048,512]{1,0:T(8,128)(2,1)}, s32[16,1,128]{2,1,0:T(1,128)}, s32[1,2048]{1,0:T(1,128)}) custom-call(s32[2048,1]{1,0:T(8,128)} %copy.20.col_ref, s32[1,2048]{1,0:T(1,128)} %bitcast.16, bf16[2048,512]{1,0:T(8,128)(2,1)} %x_ref.1), custom_call_target="tpu_custom_call" | custom-call | tf_op jit(solution)/shard_map/pack/pallas_call | solution.py:87
  14.5 0.0 copy-start.1
  14.5 0.0 copy-start.2
  14.5 41.2 %exchange_ids.1 = (bf16[64,32,512]{2,1,0:T(8,128)(2,1)}, s32[64,1,128]{2,1,0:T(1,128)}) custom-call(bf16[64,32,512]{2,1,0:T(8,128)(2,1)} %bitcast.12, s32[16,1,128]{2,1,0:T(1,128)} %get-tuple-element.15.refs_1_), custom_call_target="tpu_custom_call" | custom-call | tf_op jit(solution)/shard_map/exchange_ids/pallas_call | solution.py:179
  55.7 0.5 broadcast.55
  56.2 1.6 fusion.9
  57.8 0.7 sub.54.row_ref
  58.4 9.7 %place.1 = (bf16[2048,512]{1,0:T(8,128)(2,1)}, bf16[2048,512]{1,0:T(8,128)(2,1)}, bf16[256,512]{1,0:T(8,128)(2,1)}) custom-call(s32[1,2048]{1,0:T(1,128)} %sub.54.row_ref, bf16[2048,512]{1,0:T(8,128)(2,1)} %bitcast.11, f32[1,512]{1,0:T(1,128)} %bitcast.18), custom_call_target="tpu_custom_call" | custom-call | tf_op jit(solution)/shard_map/place/pallas_call | solution.py:205
  68.1 0.0 copy-done.1
  68.1 0.1 copy.21
  68.2 0.6 fusion.6.chosen_ref
  68.8 0.0 copy-done.2
  68.8 0.1 broadcast_in_dim.3
  68.9 0.7 reshape_reshape.3.scale_ref
  69.6 42.7 %attention.1.res_ref = bf16[2048,512]{1,0:T(8,128)(2,1)} custom-call(s32[8,4]{1,0:T(8,128)} %fusion.6.chosen_ref, bf16[2048,512]{1,0:T(8,128)(2,1)} %get-tuple-element.18.normed_ref, bf16[2048,512]{1,0:T(8,128)(2,1)} %get-tuple-element.19.grouped_ref, bf16[8,32,512]{2,1,0:T(8,128)(2,1)} %bitcast.13, bf16[512,512]{1,0:T(8,128)(2,1)} %wq_ref.1, ...), custom_call_target="tpu_custom_call" | custom-call | tf_op jit(solution)/shard_map/attention/pallas_call | solution.py:360
  112.3 2.1 %sub.55.col_ref = s32[2048,1]{1,0:T(8,128)} reshape(s32[64,32]{1,0:T(8,128)S(1)} %get-tuple-element.21) | data formatting | bytes 16384 | tf_op jit(solution)/shard_map/sub | solution.py:487
  114.3 0.0 copy-start
  114.3 42.1 %finish.1 = bf16[64,32,512]{2,1,0:T(8,128)(2,1)} custom-call(s32[2048,1]{1,0:T(8,128)} %sub.55.col_ref, bf16[2048,512]{1,0:T(8,128)(2,1)} %attention.1.res_ref, bf16[512,1024]{1,0:T(8,128)(2,1)} %wg_ref.1, bf16[512,1024]{1,0:T(8,128)(2,1)} %wu_ref.1, bf16[1024,512]{1,0:T(8,128)(2,1)} %wd_ref.1, f32[1,512]{1,0:T(1,128)} %bitcast.19), custom_call_target="tpu_custom_call" | custom-call | tf_op jit(solution)/shard_map/finish/pallas_call | solution.py:443
  156.4 0.0 copy-done
  156.4 1.4 copy.26.col_ref
  157.8 9.2 %pick.1 = bf16[2048,512]{1,0:T(8,128)(2,1)} custom-call(s32[2048,1]{1,0:T(8,128)} %copy.26.col_ref, bf16[2048,512]{1,0:T(8,128)(2,1)} %bitcast.10), custom_call_target="tpu_custom_call" | custom-call | tf_op jit(solution)/shard_map/pick/pallas_call | solution.py:466
  (1 shorter events, 0.0 us)
Async XLA Ops:
  14.5 53.6 %copy-start.1 = (s32[8,4]{0,1:T(4,128)S(1)}, s32[8,4]{0,1:T(4,128)}, u32[]{:S(2)}) copy-start(s32[8,4]{0,1:T(4,128)} %param.17) | copy-start | bytes 388
  14.5 54.3 %copy-start.2 = (f32[16]{0:T(128)S(1)}, f32[16]{0:T(128)}, u32[]{:S(2)}) copy-start(f32[16]{0:T(128)} %param.24) | copy-start | bytes 196
  114.3 42.1 %copy-start = (s32[1,2048]{1,0:T(1,128)S(1)}, s32[1,2048]{1,0:T(1,128)}, u32[]{:S(2)}) copy-start(s32[1,2048]{1,0:T(1,128)} %get-tuple-element.13) | copy-start | bytes 24580

commit v3 on v2

v3 whole, which is shorter than its diff:
```python
import functools
import math

import jax
import jax.numpy as jnp
from jax import lax
from jax.experimental import pallas as pl
from jax.experimental.pallas import tpu as pltpu
from jax.sharding import PartitionSpec as P

BALL = 256
POOL = 8
OWNERS = 4
D = 512
HEADS = 16
HD = 32
FF = 1024
ROWS = 2048
PEERS = 64
EACH = 32
CK = BALL // POOL
KEYS = BALL + OWNERS * CK
GROUP = 8
NB = ROWS // BALL
STRIDE = 13
INVERSE = 5
CHIPS = PEERS // 2
MESH = pl.DeviceIdType.MESH
F32 = jnp.float32
BF16 = jnp.bfloat16
VMEM_LIMIT = 56 * 1024 * 1024


def vmem(n):
    return [pl.BlockSpec(memory_space=pltpu.VMEM)] * n


def mm(a, b):
    return jnp.dot(a, b, preferred_element_type=F32)


def mm_nt(a, b):
    return lax.dot_general(a, b, (((1,), (1,)), ((), ())), preferred_element_type=F32)


def one_hot_rows(start, count, row):
    ids = lax.broadcasted_iota(jnp.int32, (count, row.shape[1]), 0) + start
    return jnp.where(ids == row, 1.0, 0.0).astype(BF16)


def one_hot_cols(start, col, width):
    ids = lax.broadcasted_iota(jnp.int32, (col.shape[0], width), 1) + start
    return jnp.where(ids == col, 1.0, 0.0).astype(BF16)


def column(row):
    wide = jnp.broadcast_to(row.astype(F32), (8, row.shape[1]))
    return wide.T[:, :1].astype(jnp.int32)


def ahead(k):
    return (lax.axis_index("pts") + STRIDE * k) % PEERS


def behind(k):
    return (lax.axis_index("pts") + PEERS * STRIDE - STRIDE * k) % PEERS


def greet():
    barrier = pltpu.get_barrier_semaphore()

    def signal(k, carry):
        pl.semaphore_signal(barrier, inc=1, device_id={"pts": ahead(k)}, device_id_type=MESH)
        return carry

    lax.fori_loop(1, PEERS, signal, 0)


def met():
    pl.semaphore_wait(pltpu.get_barrier_semaphore(), PEERS - 1)


def steps(lo, hi, body):
    def step(k, carry):
        body(k)
        return carry

    lax.fori_loop(lo, hi, step, 0)


def front_kernel(
    row_ref, x_ref, gain_ref, grouped_ref, normed_ref, pooled_ref, pos_ref, slot_ref,
    col, ready, numbers, landed, landed_numbers, send, recv, nsend, nrecv, here,
):
    me = lax.axis_index("pts")
    greet()
    row = row_ref[...]
    col[...] = column(row)

    def count(j, acc):
        part = col[pl.ds(pl.multiple_of(j * 256, 256), 256), :]
        less = jnp.where(part < row, 1.0, 0.0)
        return acc + jnp.sum(less.reshape(32, 8, ROWS), axis=0)

    acc = lax.fori_loop(0, NB, count, jnp.zeros((8, ROWS), F32))
    rank = jnp.sum(acc, axis=0, keepdims=True).astype(jnp.int32)
    turn = (((rank >> 5) + PEERS - me) * INVERSE) & (PEERS - 1)
    pos_ref[...] = turn * EACH + (rank & (EACH - 1))
    slot = row & (ROWS - 1)
    parts = jnp.concatenate(
        [(slot >> 6).astype(F32), (slot & 63).astype(F32), jnp.zeros((6, ROWS), F32)],
        axis=0).astype(BF16)

    def rows(k):
        return pltpu.make_async_remote_copy(
            src_ref=ready.at[k], dst_ref=landed.at[k], send_sem=send.at[k],
            recv_sem=recv.at[k], device_id={"pts": ahead(k)}, device_id_type=MESH)

    def ids(k):
        return pltpu.make_async_remote_copy(
            src_ref=numbers.at[k // 4], dst_ref=landed_numbers.at[k], send_sem=nsend.at[k],
            recv_sem=nrecv.at[k], device_id={"pts": ahead(k)}, device_id_type=MESH)

    def start(k):
        ids(k).start()
        rows(k).start()

    def prepare(c):
        hot = one_hot_rows(c * 256, 256, pos_ref[...])
        ready[pl.ds(pl.multiple_of(c * 8, 8), 8)] = mm(hot, x_ref[...]).astype(BF16).reshape(
            8, EACH, D)
        back = mm_nt(parts, hot)
        whole = (back[0:1] * 64.0 + back[1:2]).astype(jnp.int32)
        numbers[2 * c] = whole[:, :128]
        numbers[2 * c + 1] = whole[:, 128:]

    prepare(0)
    met()
    own = pltpu.make_async_copy(ready.at[0], landed.at[0], here.at[0])
    own_ids = pltpu.make_async_copy(numbers.at[0], landed_numbers.at[0], here.at[1])

    def more(c):
        prepare(c)
        first = c * 8 - 8
        steps(jnp.maximum(first, 1), first + 8, start)

    steps(1, NB, more)
    own.start()
    own_ids.start()
    steps(PEERS - 8, PEERS, start)
    own.wait()
    own_ids.wait()

    def place(c, first):
        def arrive(k):
            ids(k).wait_recv()
            rows(k).wait_recv()

        steps(1 if first else c * 8, c * 8 + 8, arrive)
        got = landed_numbers[pl.ds(pl.multiple_of(c * 8, 8), 8)]
        lane = lax.broadcasted_iota(jnp.int32, got.shape, 2) // EACH
        turn = lax.broadcasted_iota(jnp.int32, got.shape, 0) & 3
        got = jnp.where(lane == turn, got, 0)
        halves = [got[0] + got[1] + got[2] + got[3], got[4] + got[5] + got[6] + got[7]]
        number = jnp.concatenate(halves, axis=1)
        slot_ref[c] = number
        chunk = landed[pl.ds(pl.multiple_of(c * 8, 8), 8)].reshape(256, D)
        for b in range(NB):
            at = slice(b * BALL, (b + 1) * BALL)
            part = mm(one_hot_rows(b * BALL, BALL, number), chunk).astype(BF16)
            if first:
                grouped_ref[at, :] = part
            else:
                grouped_ref[at, :] = grouped_ref[at, :] + part

    place(0, True)
    steps(1, NB, lambda c: place(c, False))

    r = lax.broadcasted_iota(jnp.int32, (CK, BALL), 0)
    c = lax.broadcasted_iota(jnp.int32, (CK, BALL), 1)
    pool = jnp.where(c // POOL == r, 1.0 / POOL, 0.0).astype(BF16)

    def norm(b):
        at = pl.ds(pl.multiple_of(b * BALL, BALL), BALL)
        wide = grouped_ref[at, :].astype(F32)
        mean = jnp.mean(wide * wide, axis=-1, keepdims=True)
        normed = (wide * lax.rsqrt(mean + 1e-5) * gain_ref[...]).astype(BF16)
        normed_ref[at, :] = normed
        pooled_ref[b] = mm(pool, normed).astype(BF16)

    steps(0, NB, norm)

    def sent(k):
        ids(k).wait_send()
        rows(k).wait_send()

    steps(1, PEERS, sent)


def front(row, x, gain):
    return pl.pallas_call(
        front_kernel,
        in_specs=vmem(3),
        out_specs=vmem(5),
        out_shape=[
            jax.ShapeDtypeStruct((ROWS, D), BF16),
            jax.ShapeDtypeStruct((ROWS, D), BF16),
            jax.ShapeDtypeStruct((NB, CK, D), BF16),
            jax.ShapeDtypeStruct((1, ROWS), jnp.int32),
            jax.ShapeDtypeStruct((NB, 1, 256), jnp.int32),
        ],
        scratch_shapes=[
            pltpu.VMEM((ROWS, 1), jnp.int32),
            pltpu.VMEM((PEERS, EACH, D), BF16),
            pltpu.VMEM((16, 1, 128), jnp.int32),
            pltpu.VMEM((PEERS, EACH, D), BF16),
            pltpu.VMEM((PEERS, 1, 128), jnp.int32),
            pltpu.SemaphoreType.DMA((PEERS,)),
            pltpu.SemaphoreType.DMA((PEERS,)),
            pltpu.SemaphoreType.DMA((PEERS,)),
            pltpu.SemaphoreType.DMA((PEERS,)),
            pltpu.SemaphoreType.DMA((2,)),
        ],
        compiler_params=pltpu.CompilerParams(
            collective_id=0, has_side_effects=True, vmem_limit_bytes=VMEM_LIMIT),
        name="front",
    )(row, x, gain)


def head_norm_cols(u):
    shaped = u.reshape(HEADS, HD, u.shape[1])
    mean = jnp.mean(shaped * shaped, axis=1, keepdims=True)
    return (shaped * lax.rsqrt(mean + 1e-6)).astype(BF16)


def block_ones(rows, per_row, per_col, value):
    a = lax.broadcasted_iota(jnp.int32, (rows, 256), 0) // per_row
    b = lax.broadcasted_iota(jnp.int32, (rows, 256), 1) // per_col
    return jnp.where(a == b, value, 0.0).astype(BF16)


def set_heads(keys, values, key, value, count):
    lane = lax.broadcasted_iota(jnp.int32, (1, 128), 1) // HD
    zero = jnp.zeros((), BF16)
    for h in range(HEADS):
        g, l = h // GROUP, h % GROUP
        t = l // 4
        at = slice(l * count, (l + 1) * count)
        keys[g, l * HD:(l + 1) * HD, at] = key[h]
        cols = slice(g * 256 + t * 128, g * 256 + t * 128 + 128)
        values[g, at, t * 128:(t + 1) * 128] = jnp.where(lane == (l % 4), value[:, cols], zero)


def attention_kernel(
    chosen_ref, normed_ref, grouped_ref, pooled_ref, wq_ref, wk_ref, wv_ref, wpk_ref,
    wpv_ref, wo_ref, scale_ref, out_ref,
    cand, near_keys, near_values, far_keys, far_values, probs, partial, queries,
    totals, sums, wk_t, wpk_t, mix, spread, send, recv, here,
):
    me = lax.axis_index("pts")
    core = me % 2
    chip = me // 2
    partner = chip * 2 + 1 - core
    steps = (1, -1, 2, -2)

    def chip_at(e):
        return ((chip + e + CHIPS) % CHIPS) * 2 + core

    barrier = pltpu.get_barrier_semaphore()
    for d in [partner] + [chip_at(e) for e in steps]:
        pl.semaphore_signal(barrier, inc=1, device_id={"pts": d}, device_id_type=MESH)
    pl.semaphore_wait(barrier, 1 + len(steps))

    def block(slot):
        return cand.at[pl.ds(slot * NB, NB)]

    def remote(src, slot, at, d):
        return pltpu.make_async_remote_copy(
            src_ref=src, dst_ref=block(slot), send_sem=send.at[at], recv_sem=recv.at[at],
            device_id={"pts": d}, device_id_type=MESH)

    outs = [remote(pooled_ref, (2 - e) * 2 + core, 1 + i, chip_at(e))
            for i, e in enumerate(steps)]
    for copy in outs:
        copy.start()
    to_partner = remote(pooled_ref, 4 + core, 0, partner)
    to_partner.start()
    own = pltpu.make_async_copy(pooled_ref, block(4 + core), here.at[0])
    own.start()
    onward = [remote(block((2 - e) * 2 + core), (2 - e) * 2 + core, 5 + i, partner)
              for i, e in enumerate(steps)]

    for ref in (near_keys, near_values, far_keys, far_values):
        ref[...] = jnp.zeros_like(ref)
    wk_t[...] = wk_ref[...].T
    wpk_t[...] = wpk_ref[...].T
    mix[...] = block_ones(256, HD, HD, 1.0 / HD)
    spread[...] = block_ones(GROUP * 128, 128, HD, 1.0)

    def near(ball, carry):
        for at, pair in ((5, (0, 1)), (7, (2, 3))):
            @pl.when(ball == at)
            def _():
                for i in pair:
                    outs[i].wait_recv()
                    onward[i].start()

        rows = pl.ds(pl.multiple_of(ball * BALL, BALL), BALL)
        normed = normed_ref[rows, :]
        q = mm(normed, wq_ref[...])
        square = (q * q).astype(BF16)
        mean = jnp.concatenate(
            [mm(square[:, :256], mix[...]), mm(square[:, 256:], mix[...])], axis=1)
        query = (q * lax.rsqrt(mean + 1e-6) * scale_ref[...]).astype(BF16)
        queries[rows, :] = query
        key = head_norm_cols(mm_nt(wk_t[...], normed))
        value = mm(normed, wv_ref[...]).astype(BF16)
        set_heads(near_keys, near_values, key, value, BALL)
        for g in range(HEADS // GROUP):
            cols = slice(g * 256, (g + 1) * 256)
            qg = query[:, cols]
            for l in range(GROUP):
                p = jnp.exp2(mm(qg, near_keys[g, :, l * BALL:(l + 1) * BALL]))
                probs[:, l * BALL:(l + 1) * BALL] = p.astype(BF16)
                partial[:, l * 128:(l + 1) * 128] = (p[:, :128] + p[:, 128:]).astype(BF16)
            totals[rows, cols] = mm(probs[...], near_values[g])
            sums[rows, cols] = mm(partial[...], spread[...])
        return carry

    lax.fori_loop(0, NB, near, 0)
    own.wait()
    to_partner.wait()
    for copy in outs:
        copy.wait_send()
    for copy in onward:
        copy.wait()

    def far(ball, carry):
        rows = pl.ds(pl.multiple_of(ball * BALL, BALL), BALL)
        picked = []
        for j in range(OWNERS):
            picked.append(cand[chosen_ref[ball, j]])
        picked = jnp.concatenate(picked, axis=0)
        key = head_norm_cols(mm_nt(wpk_t[...], picked))
        value = mm(picked, wpv_ref[...]).astype(BF16)
        set_heads(far_keys, far_values, key, value, OWNERS * CK)
        attended = []
        for g in range(HEADS // GROUP):
            cols = slice(g * 256, (g + 1) * 256)
            qg = queries[rows, cols]
            for l in range(GROUP // 2):
                p = jnp.exp2(mm(qg, far_keys[g, :, l * 256:(l + 1) * 256]))
                partial[:, l * 256:(l + 1) * 256] = p.astype(BF16)
            total = totals[rows, cols] + mm(partial[...], far_values[g])
            denominator = sums[rows, cols] + mm(partial[...], spread[...])
            attended.append((total / denominator).astype(BF16))
        attended = jnp.concatenate(attended, axis=1)
        out_ref[rows, :] = (
            grouped_ref[rows, :].astype(F32) + mm(attended, wo_ref[...])).astype(BF16)
        return carry

    lax.fori_loop(0, NB, far, 0)


def attention(chosen, arrays):
    return pl.pallas_call(
        attention_kernel,
        in_specs=[pl.BlockSpec(memory_space=pltpu.SMEM)] + vmem(len(arrays)),
        out_specs=vmem(1)[0],
        out_shape=jax.ShapeDtypeStruct((ROWS, D), BF16),
        scratch_shapes=[
            pltpu.VMEM((10 * NB, CK, D), BF16),
            pltpu.VMEM((2, 256, GROUP * BALL), BF16),
            pltpu.VMEM((2, GROUP * BALL, 256), BF16),
            pltpu.VMEM((2, 256, GROUP * 128), BF16),
            pltpu.VMEM((2, GROUP * 128, 256), BF16),
            pltpu.VMEM((BALL, GROUP * BALL), BF16),
            pltpu.VMEM((BALL, GROUP * 128), BF16),
            pltpu.VMEM((ROWS, D), BF16),
            pltpu.VMEM((ROWS, D), F32),
            pltpu.VMEM((ROWS, D), F32),
            pltpu.VMEM((D, D), BF16),
            pltpu.VMEM((D, D), BF16),
            pltpu.VMEM((256, 256), BF16),
            pltpu.VMEM((GROUP * 128, 256), BF16),
            pltpu.SemaphoreType.DMA((9,)),
            pltpu.SemaphoreType.DMA((9,)),
            pltpu.SemaphoreType.DMA((1,)),
        ],
        compiler_params=pltpu.CompilerParams(
            collective_id=2, has_side_effects=True, vmem_limit_bytes=VMEM_LIMIT),
        name="attention",
    )(chosen, *arrays)


def finish_kernel(slot_ref, pos_ref, res_ref, wg_ref, wu_ref, wd_ref, gain_ref, out_ref,
                  col, ready, landed, send, recv, here):
    greet()

    def back(k):
        return pltpu.make_async_remote_copy(
            src_ref=ready.at[k], dst_ref=landed.at[k], send_sem=send.at[k],
            recv_sem=recv.at[k], device_id={"pts": behind(k)}, device_id_type=MESH)

    own = pltpu.make_async_copy(ready.at[0], landed.at[0], here.at[0])

    def prepare(c):
        hot = one_hot_cols(0, column(slot_ref[c]), ROWS)
        wide = mm(hot, res_ref[...])
        mean = jnp.mean(wide * wide, axis=-1, keepdims=True)
        ffn = (wide * lax.rsqrt(mean + 1e-5) * gain_ref[...]).astype(BF16)
        gate = mm(ffn, wg_ref[...])
        up = mm(ffn, wu_ref[...])
        hidden = (gate / (1.0 + jnp.exp(-gate)) * up).astype(BF16)
        result = (wide + mm(hidden, wd_ref[...])).astype(BF16)
        ready[pl.ds(pl.multiple_of(c * 8, 8), 8)] = result.reshape(8, EACH, D)

    prepare(0)
    met()

    def more(c):
        prepare(c)
        first = c * 8 - 8
        steps(jnp.maximum(first, 1), first + 8, lambda k: back(k).start())

    steps(1, NB, more)
    own.start()
    steps(PEERS - 8, PEERS, lambda k: back(k).start())
    col[...] = column(pos_ref[...])
    own.wait()

    def place(c, first):
        steps(1 if first else c * 8, c * 8 + 8, lambda k: back(k).wait_recv())
        chunk = landed[pl.ds(pl.multiple_of(c * 8, 8), 8)].reshape(256, D)
        for b in range(NB):
            at = slice(b * 256, (b + 1) * 256)
            part = mm(one_hot_cols(c * 256, col[at, :], 256), chunk).astype(BF16)
            if first:
                out_ref[at, :] = part
            else:
                out_ref[at, :] = out_ref[at, :] + part

    place(0, True)
    steps(1, NB, lambda c: place(c, False))
    steps(1, PEERS, lambda k: back(k).wait_send())


def finish(*arrays):
    return pl.pallas_call(
        finish_kernel,
        in_specs=vmem(len(arrays)),
        out_specs=vmem(1)[0],
        out_shape=jax.ShapeDtypeStruct((ROWS, D), BF16),
        scratch_shapes=[
            pltpu.VMEM((ROWS, 1), jnp.int32),
            pltpu.VMEM((PEERS, EACH, D), BF16),
            pltpu.VMEM((PEERS, EACH, D), BF16),
            pltpu.SemaphoreType.DMA((PEERS,)),
            pltpu.SemaphoreType.DMA((PEERS,)),
            pltpu.SemaphoreType.DMA((1,)),
        ],
        compiler_params=pltpu.CompilerParams(
            collective_id=1, has_side_effects=True, vmem_limit_bytes=VMEM_LIMIT),
        name="finish",
    )(*arrays)


def on_device(
    points, point_row_index, neighbour_ball_list, attention_norm_gain, query_weight,
    key_weight, value_weight, pooled_key_weight, pooled_value_weight, head_score_scale,
    output_weight, feedforward_norm_gain, gate_weight, up_weight, down_weight,
):
    me = lax.axis_index("pts")
    grouped, normed, pooled, pos, slot = front(
        point_row_index.reshape(1, ROWS), points, attention_norm_gain.reshape(1, D))
    owner = neighbour_ball_list // NB
    place_of = jnp.mod(owner // 2 - me // 2 + 2, CHIPS) * 2 + owner % 2
    chosen = place_of * NB + neighbour_ball_list % NB
    scale = jnp.repeat(head_score_scale * (math.log2(math.e) / HD), HD).reshape(1, D)
    residual = attention(
        chosen,
        (normed, grouped, pooled, query_weight, key_weight, value_weight, pooled_key_weight,
         pooled_value_weight, output_weight, scale))
    return finish(slot, pos, residual, gate_weight, up_weight, down_weight,
                  feedforward_norm_gain.reshape(1, D))


def solution(mesh):
    return jax.shard_map(
        on_device,
        mesh=mesh,
        in_specs=(
            P(("rep", "pts"), None), P(("rep", "pts")), P(("rep", "pts"), None),
            P(), P(), P(), P(), P(), P(), P(), P(), P(), P(), P(), P(),
        ),
        out_specs=P(("rep", "pts"), None),
        check_vma=False,
    )
```

time: 170 us -> 144 us (0.85); the launches traced: 167 us -> 144 us
  Pallas kernels: 157 us -> 138 us
  local copies, waits for them, and re-layouts: 7.48 us -> 4.49 us
    pallas_call x4 -> x1, Pallas kernels: 72.5 us -> 48.8 us  [front(): pl.pallas_call(front_kernel, in_specs=vmem(3), out_specs=vmem(5), out_sha...]
    pallas_call x1, Pallas kernels: 42.1 us -> 48.9 us  [finish(): pl.pallas_call(finish_kernel, in_specs=vmem(len(arrays)), out_specs=vmem(...]
    unnamed x7 -> x2, local copies, waits for them, and re-layouts: 0.09 us -> 3.8 us
    reshape x2 -> x0, local copies, waits for them, and re-layouts: 3.4 us -> none  [the longest x1 2.03 us: on_device(): point_row_index.reshape(ROWS, 1)]
    sub x3 -> x0, local copies, waits for them, and re-layouts: 3.24 us -> none  [on_device(): slot = mine.reshape(ROWS) - me * ROWS]
    pallas_call x1, Pallas kernels: 42.7 us -> 40.4 us  [attention(): pl.pallas_call(attention_kernel, in_specs=[pl.BlockSpec(memory_space=pltp...]
where the time goes in v3:
time: 144 us
  Pallas kernels  138 us (96%)
  local copies, waits for them, and re-layouts  4.49 us (3%)
    pallas_call x1, Pallas kernels, finish(): pl.pallas_call(finish_kernel, in_specs=vmem(len(arrays)), out_specs=vmem(...  48.9 us
    pallas_call x1, Pallas kernels, front(): pl.pallas_call(front_kernel, in_specs=vmem(3), out_specs=vmem(5), out_sha...  48.8 us
    pallas_call x1, Pallas kernels, attention(): pl.pallas_call(attention_kernel, in_specs=[pl.BlockSpec(memory_space=pltp...  40.4 us
    unnamed x2, local copies, waits for them, and re-layouts  3.8 us

profile of v3, /device:TPU:1, one launch (start us, length us, event | category | flops | bytes accessed | tf_op | source)
XLA Modules:
  0.0 143.8 jit_solution(15517751787930553433)
XLA Ops:
  0.0 0.7 broadcast_multiply_fusion
  0.7 0.8 copy.16
  1.4 0.6 fusion.6.chosen_ref
  2.0 0.1 broadcast_in_dim.3
  2.1 0.6 reshape_reshape.3.scale_ref
  2.7 48.8 %front.1 = (bf16[2048,512]{1,0:T(8,128)(2,1)}, bf16[2048,512]{1,0:T(8,128)(2,1)}, bf16[8,32,512]{2,1,0:T(8,128)(2,1)}, s32[1,2048]{1,0:T(1,128)}, s32[8,1,256]{2,1,0:T(1,128)}) custom-call(s32[1,2048]{1,0:T(1,128)} %bitcast.3, bf16[2048,512]{1,0:T(8,128)(2,1)} %x_ref.1, f32[1,512]{1,0:T(1,128)} %bitcast.4), custom_call_target="tpu_custom_call" | custom-call | tf_op jit(solution)/shard_map/front/pallas_call | solution.py:201
  51.6 40.4 %attention.1.res_ref = bf16[2048,512]{1,0:T(8,128)(2,1)} custom-call(s32[8,4]{1,0:T(8,128)} %fusion.6.chosen_ref, bf16[2048,512]{1,0:T(8,128)(2,1)} %get-tuple-element.12.normed_ref, bf16[2048,512]{1,0:T(8,128)(2,1)} %get-tuple-element.13.grouped_ref, bf16[8,32,512]{2,1,0:T(8,128)(2,1)} %get-tuple-element.14.pooled_ref, bf16[512,512]{1,0:T(8,128)(2,1)} %wq_ref.1, ...), custom_call_target="tpu_custom_call" | custom-call | tf_op jit(solution)/shard_map/attention/pallas_call | solution.py:366
  91.9 48.9 %finish.1 = bf16[2048,512]{1,0:T(8,128)(2,1)} custom-call(s32[8,1,256]{2,1,0:T(1,128)} %get-tuple-element.10.slot_ref, s32[1,2048]{1,0:T(1,128)} %get-tuple-element.11.pos_ref, bf16[2048,512]{1,0:T(8,128)(2,1)} %attention.1.res_ref, bf16[512,1024]{1,0:T(8,128)(2,1)} %wg_ref.1, bf16[512,1024]{1,0:T(8,128)(2,1)} %wu_ref.1, bf16[1024,512]{1,0:T(8,128)(2,1)} %wd_ref.1, ...), custom_call_target="tpu_custom_call" | custom-call | tf_op jit(solution)/shard_map/finish/pallas_call | solution.py:449
  140.8 3.0 %copy.21 = bf16[2048,512]{1,0:T(8,128)(2,1)} copy(bf16[2048,512]{1,0:T(8,128)(2,1)} %finish.1) | data formatting | bytes 4194304

commit v4 on v3

--- a/solution.py
+++ b/solution.py
@@ -19,10 +19,9 @@
 PEERS = 64
 EACH = 32
 CK = BALL // POOL
-KEYS = BALL + OWNERS * CK
-GROUP = 8
 NB = ROWS // BALL
 STRIDE = 13
+LAG = 16
 INVERSE = 5
 CHIPS = PEERS // 2
 MESH = pl.DeviceIdType.MESH
@@ -227,10 +226,10 @@
     )(row, x, gain)
 
 
-def head_norm_cols(u):
-    shaped = u.reshape(HEADS, HD, u.shape[1])
-    mean = jnp.mean(shaped * shaped, axis=1, keepdims=True)
-    return (shaped * lax.rsqrt(mean + 1e-6)).astype(BF16)
+def head_norm_rows(u, mix):
+    square = (u * u).astype(BF16)
+    mean = jnp.concatenate([mm(square[:, :256], mix), mm(square[:, 256:], mix)], axis=1)
+    return (u * lax.rsqrt(mean + 1e-6)).astype(BF16)
 
 
 def block_ones(rows, per_row, per_col, value):
@@ -239,37 +238,47 @@
     return jnp.where(a == b, value, 0.0).astype(BF16)
 
 
-def set_heads(keys, values, key, value, count):
-    lane = lax.broadcasted_iota(jnp.int32, (1, 128), 1) // HD
-    zero = jnp.zeros((), BF16)
+def set_queries(spread, query):
     for h in range(HEADS):
-        g, l = h // GROUP, h % GROUP
-        t = l // 4
-        at = slice(l * count, (l + 1) * count)
-        keys[g, l * HD:(l + 1) * HD, at] = key[h]
-        cols = slice(g * 256 + t * 128, g * 256 + t * 128 + 128)
-        values[g, at, t * 128:(t + 1) * 128] = jnp.where(lane == (l % 4), value[:, cols], zero)
+        at = (h % 4) * HD
+        spread[h, at:at + HD, :] = query[h]
+
+
+def head_sums(key, value, spread, probs, finish_head):
+    ones = jnp.ones((16, value.shape[1]), BF16)
+    count = value.shape[1]
+
+    def scores(h):
+        group = slice((h // 4) * 128, (h // 4) * 128 + 128)
+        probs[h % LAG, :count, :] = jnp.exp2(mm(key[:, group], spread[h])).astype(BF16)
+
+    def weigh(h):
+        rows = jnp.concatenate([value[h * HD:(h + 1) * HD, :], ones], axis=0)
+        finish_head(h, mm(rows, probs[h % LAG, :count, :])[:HD + 8])
+
+    for h in range(HEADS + LAG - 1):
+        if h < HEADS:
+            scores(h)
+        if h >= LAG - 1:
+            weigh(h - LAG + 1)
 
 
 def attention_kernel(
-    chosen_ref, normed_ref, grouped_ref, pooled_ref, wq_ref, wk_ref, wv_ref, wpk_ref,
-    wpv_ref, wo_ref, scale_ref, out_ref,
-    cand, near_keys, near_values, far_keys, far_values, probs, partial, queries,
-    totals, sums, wk_t, wpk_t, mix, spread, send, recv, here,
+    chosen_ref, scale_ref, normed_ref, grouped_ref, pooled_ref, wq_ref, wk_ref, wv_ref,
+    wpk_ref, wpv_ref, wo_ref, out_ref,
+    cand, spread, queries, totals, probs, turned, wqv_t, wpv_t, mix, send, recv, here,
 ):
     me = lax.axis_index("pts")
     core = me % 2
     chip = me // 2
     partner = chip * 2 + 1 - core
-    steps = (1, -1, 2, -2)
-
     def chip_at(e):
         return ((chip + e + CHIPS) % CHIPS) * 2 + core
 
     barrier = pltpu.get_barrier_semaphore()
-    for d in [partner] + [chip_at(e) for e in steps]:
+    for d in (partner, chip_at(1), chip_at(-1)):
         pl.semaphore_signal(barrier, inc=1, device_id={"pts": d}, device_id_type=MESH)
-    pl.semaphore_wait(barrier, 1 + len(steps))
+    pl.semaphore_wait(barrier, 3)
 
     def block(slot):
         return cand.at[pl.ds(slot * NB, NB)]
@@ -279,58 +288,63 @@
             src_ref=src, dst_ref=block(slot), send_sem=send.at[at], recv_sem=recv.at[at],
             device_id={"pts": d}, device_id_type=MESH)
 
-    outs = [remote(pooled_ref, (2 - e) * 2 + core, 1 + i, chip_at(e))
-            for i, e in enumerate(steps)]
+    def slot(e):
+        return (2 - e) * 2 + core
+
+    outs = [remote(pooled_ref, slot(e), 1 + i, chip_at(e)) for i, e in enumerate((1, -1))]
     for copy in outs:
         copy.start()
-    to_partner = remote(pooled_ref, 4 + core, 0, partner)
+    to_partner = remote(pooled_ref, slot(0), 0, partner)
     to_partner.start()
-    own = pltpu.make_async_copy(pooled_ref, block(4 + core), here.at[0])
+    own = pltpu.make_async_copy(pooled_ref, block(slot(0)), here.at[0])
     own.start()
-    onward = [remote(block((2 - e) * 2 + core), (2 - e) * 2 + core, 5 + i, partner)
-              for i, e in enumerate(steps)]
-
-    for ref in (near_keys, near_values, far_keys, far_values):
-        ref[...] = jnp.zeros_like(ref)
-    wk_t[...] = wk_ref[...].T
-    wpk_t[...] = wpk_ref[...].T
+    farther = [remote(block(slot(e)), slot(2 * e), 3 + i, chip_at(e))
+               for i, e in enumerate((1, -1))]
+    onward = [remote(block(slot(e)), slot(e), 5 + i, partner)
+              for i, e in enumerate((1, -1, 2, -2))]
+
+    spread[...] = jnp.zeros_like(spread)
+    wqv_t[:D, :] = wq_ref[...].T
+    wqv_t[D:, :] = wv_ref[...].T
+    wpv_t[...] = wpv_ref[...].T
     mix[...] = block_ones(256, HD, HD, 1.0 / HD)
-    spread[...] = block_ones(GROUP * 128, 128, HD, 1.0)
 
     def near(ball, carry):
-        for at, pair in ((5, (0, 1)), (7, (2, 3))):
-            @pl.when(ball == at)
-            def _():
-                for i in pair:
-                    outs[i].wait_recv()
-                    onward[i].start()
+        @pl.when(ball == 4)
+        def _():
+            for i in range(2):
+                outs[i].wait_recv()
+                farther[i].start()
+                onward[i].start()
+
+        @pl.when(ball == 7)
+        def _():
+            for i in range(2):
+                farther[i].wait_recv()
+                onward[2 + i].start()
 
         rows = pl.ds(pl.multiple_of(ball * BALL, BALL), BALL)
         normed = normed_ref[rows, :]
-        q = mm(normed, wq_ref[...])
-        square = (q * q).astype(BF16)
-        mean = jnp.concatenate(
-            [mm(square[:, :256], mix[...]), mm(square[:, 256:], mix[...])], axis=1)
-        query = (q * lax.rsqrt(mean + 1e-6) * scale_ref[...]).astype(BF16)
-        queries[rows, :] = query
-        key = head_norm_cols(mm_nt(wk_t[...], normed))
-        value = mm(normed, wv_ref[...]).astype(BF16)
-        set_heads(near_keys, near_values, key, value, BALL)
-        for g in range(HEADS // GROUP):
-            cols = slice(g * 256, (g + 1) * 256)
-            qg = query[:, cols]
-            for l in range(GROUP):
-                p = jnp.exp2(mm(qg, near_keys[g, :, l * BALL:(l + 1) * BALL]))
-                probs[:, l * BALL:(l + 1) * BALL] = p.astype(BF16)
-                partial[:, l * 128:(l + 1) * 128] = (p[:, :128] + p[:, 128:]).astype(BF16)
-            totals[rows, cols] = mm(probs[...], near_values[g])
-            sums[rows, cols] = mm(partial[...], spread[...])
+        both = mm_nt(wqv_t[...], normed)
+        shaped = both[:D].reshape(HEADS, HD, BALL)
+        mean = jnp.mean(shaped * shaped, axis=1, keepdims=True)
+        factor = lax.rsqrt(mean + 1e-6)
+        for h in range(HEADS):
+            queries[ball, h] = (shaped[h] * (factor[h] * (scale_ref[h] * (math.log2(math.e) / HD)))).astype(BF16)
+        value = both[D:].astype(BF16)
+        key = head_norm_rows(mm(normed, wk_ref[...]), mix[...])
+        set_queries(spread, queries.at[ball])
+
+        def keep(h, total):
+            totals[ball, h] = total
+
+        head_sums(key, value, spread, probs, keep)
         return carry
 
     lax.fori_loop(0, NB, near, 0)
     own.wait()
     to_partner.wait()
-    for copy in outs:
+    for copy in outs + farther:
         copy.wait_send()
     for copy in onward:
         copy.wait()
@@ -341,20 +355,16 @@
         for j in range(OWNERS):
             picked.append(cand[chosen_ref[ball, j]])
         picked = jnp.concatenate(picked, axis=0)
-        key = head_norm_cols(mm_nt(wpk_t[...], picked))
-        value = mm(picked, wpv_ref[...]).astype(BF16)
-        set_heads(far_keys, far_values, key, value, OWNERS * CK)
-        attended = []
-        for g in range(HEADS // GROUP):
-            cols = slice(g * 256, (g + 1) * 256)
-            qg = queries[rows, cols]
-            for l in range(GROUP // 2):
-                p = jnp.exp2(mm(qg, far_keys[g, :, l * 256:(l + 1) * 256]))
-                partial[:, l * 256:(l + 1) * 256] = p.astype(BF16)
-            total = totals[rows, cols] + mm(partial[...], far_values[g])
-            denominator = sums[rows, cols] + mm(partial[...], spread[...])
-            attended.append((total / denominator).astype(BF16))
-        attended = jnp.concatenate(attended, axis=1)
+        key = head_norm_rows(mm(picked, wpk_ref[...]), mix[...])
+        value = mm_nt(wpv_t[...], picked).astype(BF16)
+        set_queries(spread, queries.at[ball])
+
+        def close(h, total):
+            total = totals[ball, h] + total
+            turned[h * HD:(h + 1) * HD, :] = (total[:HD] / total[HD:HD + 1]).astype(BF16)
+
+        head_sums(key, value, spread, probs, close)
+        attended = turned[...].T
         out_ref[rows, :] = (
             grouped_ref[rows, :].astype(F32) + mm(attended, wo_ref[...])).astype(BF16)
         return carry
@@ -362,27 +372,22 @@
     lax.fori_loop(0, NB, far, 0)
 
 
-def attention(chosen, arrays):
+def attention(chosen, scale, arrays):
     return pl.pallas_call(
         attention_kernel,
-        in_specs=[pl.BlockSpec(memory_space=pltpu.SMEM)] + vmem(len(arrays)),
+        in_specs=[pl.BlockSpec(memory_space=pltpu.SMEM)] * 2 + vmem(len(arrays)),
         out_specs=vmem(1)[0],
         out_shape=jax.ShapeDtypeStruct((ROWS, D), BF16),
         scratch_shapes=[
             pltpu.VMEM((10 * NB, CK, D), BF16),
-            pltpu.VMEM((2, 256, GROUP * BALL), BF16),
-            pltpu.VMEM((2, GROUP * BALL, 256), BF16),
-            pltpu.VMEM((2, 256, GROUP * 128), BF16),
-            pltpu.VMEM((2, GROUP * 128, 256), BF16),
-            pltpu.VMEM((BALL, GROUP * BALL), BF16),
-            pltpu.VMEM((BALL, GROUP * 128), BF16),
-            pltpu.VMEM((ROWS, D), BF16),
-            pltpu.VMEM((ROWS, D), F32),
-            pltpu.VMEM((ROWS, D), F32),
-            pltpu.VMEM((D, D), BF16),
+            pltpu.VMEM((HEADS, 128, BALL), BF16),
+            pltpu.VMEM((NB, HEADS, HD, BALL), BF16),
+            pltpu.VMEM((NB, HEADS, HD + 8, BALL), F32),
+            pltpu.VMEM((LAG, BALL, BALL), BF16),
+            pltpu.VMEM((D, BALL), BF16),
+            pltpu.VMEM((2 * D, D), BF16),
             pltpu.VMEM((D, D), BF16),
             pltpu.VMEM((256, 256), BF16),
-            pltpu.VMEM((GROUP * 128, 256), BF16),
             pltpu.SemaphoreType.DMA((9,)),
             pltpu.SemaphoreType.DMA((9,)),
             pltpu.SemaphoreType.DMA((1,)),
@@ -390,7 +395,7 @@
         compiler_params=pltpu.CompilerParams(
             collective_id=2, has_side_effects=True, vmem_limit_bytes=VMEM_LIMIT),
         name="attention",
-    )(chosen, *arrays)
+    )(chosen, scale, *arrays)
 
 
 def finish_kernel(slot_ref, pos_ref, res_ref, wg_ref, wu_ref, wd_ref, gain_ref, out_ref,
@@ -404,9 +409,11 @@
 
     own = pltpu.make_async_copy(ready.at[0], landed.at[0], here.at[0])
 
-    def prepare(c):
+    def prepare(c, between=None):
         hot = one_hot_cols(0, column(slot_ref[c]), ROWS)
         wide = mm(hot, res_ref[...])
+        if between is not None:
+            between()
         mean = jnp.mean(wide * wide, axis=-1, keepdims=True)
         ffn = (wide * lax.rsqrt(mean + 1e-5) * gain_ref[...]).astype(BF16)
         gate = mm(ffn, wg_ref[...])
@@ -419,9 +426,9 @@
     met()
 
     def more(c):
-        prepare(c)
         first = c * 8 - 8
-        steps(jnp.maximum(first, 1), first + 8, lambda k: back(k).start())
+        prepare(c, lambda: steps(
+            jnp.maximum(first, 1), first + 8, lambda k: back(k).start()))
 
     steps(1, NB, more)
     own.start()
@@ -429,19 +436,28 @@
     col[...] = column(pos_ref[...])
     own.wait()
 
-    def place(c, first):
-        steps(1 if first else c * 8, c * 8 + 8, lambda k: back(k).wait_recv())
+    def place(c, store):
         chunk = landed[pl.ds(pl.multiple_of(c * 8, 8), 8)].reshape(256, D)
         for b in range(NB):
             at = slice(b * 256, (b + 1) * 256)
-            part = mm(one_hot_cols(c * 256, col[at, :], 256), chunk).astype(BF16)
-            if first:
-                out_ref[at, :] = part
-            else:
-                out_ref[at, :] = out_ref[at, :] + part
-
-    place(0, True)
-    steps(1, NB, lambda c: place(c, False))
+            store(at, mm(one_hot_cols(c * 256, col[at, :], 256), chunk).astype(BF16))
+
+    def arrive(lo, hi):
+        steps(lo, hi, lambda k: back(k).wait_recv())
+
+    def set_out(at, part):
+        out_ref[at, :] = part
+
+    def add(at, part):
+        out_ref[at, :] = out_ref[at, :] + part
+
+    def middle(c):
+        arrive(c * 8, c * 8 + 8)
+        place(c, add)
+
+    arrive(1, 8)
+    place(0, set_out)
+    steps(1, NB, middle)
     steps(1, PEERS, lambda k: back(k).wait_send())
 
 
@@ -476,11 +492,10 @@
     owner = neighbour_ball_list // NB
     place_of = jnp.mod(owner // 2 - me // 2 + 2, CHIPS) * 2 + owner % 2
     chosen = place_of * NB + neighbour_ball_list % NB
-    scale = jnp.repeat(head_score_scale * (math.log2(math.e) / HD), HD).reshape(1, D)
     residual = attention(
-        chosen,
+        chosen, head_score_scale,
         (normed, grouped, pooled, query_weight, key_weight, value_weight, pooled_key_weight,
-         pooled_value_weight, output_weight, scale))
+         pooled_value_weight, output_weight))
     return finish(slot, pos, residual, gate_weight, up_weight, down_weight,
                   feedforward_norm_gain.reshape(1, D))
 

time: 144 us -> 134 us (0.931)
  Pallas kernels: 138 us -> 129 us
    pallas_call x1, Pallas kernels: 48.9 us -> 42.6 us  [finish(): pl.pallas_call(finish_kernel, in_specs=vmem(len(arrays)), out_specs=vmem(...]
    pallas_call x1, Pallas kernels: 40.4 us -> 37.7 us  [attention(): pl.pallas_call(attention_kernel, in_specs=[pl.BlockSpec(memory_space=pltp...]
where the time goes in v4:
time: 134 us
  Pallas kernels  129 us (96%)
  local copies, waits for them, and re-layouts  3.8 us (3%)
    pallas_call x1, Pallas kernels, front(): pl.pallas_call(front_kernel, in_specs=vmem(3), out_specs=vmem(5), out_sha...  48.8 us
    pallas_call x1, Pallas kernels, finish(): pl.pallas_call(finish_kernel, in_specs=vmem(len(arrays)), out_specs=vmem(...  42.6 us
    pallas_call x1, Pallas kernels, attention(): pl.pallas_call(attention_kernel, in_specs=[pl.BlockSpec(memory_space=pltp...  37.7 us
    unnamed x2, local copies, waits for them, and re-layouts  3.8 us

profile of v4, /device:TPU:1, one launch (start us, length us, event | category | flops | bytes accessed | tf_op | source)
XLA Modules:
  0.0 133.6 jit_solution(14098994538896570142)
XLA Ops:
  0.0 0.8 copy.16
  0.8 0.6 fusion.6.chosen_ref
  1.4 48.8 %front.1 = (bf16[2048,512]{1,0:T(8,128)(2,1)}, bf16[2048,512]{1,0:T(8,128)(2,1)}, bf16[8,32,512]{2,1,0:T(8,128)(2,1)}, s32[1,2048]{1,0:T(1,128)}, s32[8,1,256]{2,1,0:T(1,128)}) custom-call(s32[1,2048]{1,0:T(1,128)} %bitcast.3, bf16[2048,512]{1,0:T(8,128)(2,1)} %x_ref.1, f32[1,512]{1,0:T(1,128)} %bitcast.4), custom_call_target="tpu_custom_call" | custom-call | tf_op jit(solution)/shard_map/front/pallas_call | solution.py:200
  50.2 37.7 %attention.1.res_ref = bf16[2048,512]{1,0:T(8,128)(2,1)} custom-call(s32[8,4]{1,0:T(8,128)} %fusion.6.chosen_ref, f32[16]{0:T(128)} %scale_ref.1, bf16[2048,512]{1,0:T(8,128)(2,1)} %get-tuple-element.12.normed_ref, bf16[2048,512]{1,0:T(8,128)(2,1)} %get-tuple-element.13.grouped_ref, bf16[8,32,512]{2,1,0:T(8,128)(2,1)} %get-tuple-element.14.pooled_ref, ...), custom_call_target="tpu_custom_call" | custom-call | tf_op jit(solution)/shard_map/attention/pallas_call | solution.py:376
  87.9 42.6 %finish.1 = bf16[2048,512]{1,0:T(8,128)(2,1)} custom-call(s32[8,1,256]{2,1,0:T(1,128)} %get-tuple-element.10.slot_ref, s32[1,2048]{1,0:T(1,128)} %get-tuple-element.11.pos_ref, bf16[2048,512]{1,0:T(8,128)(2,1)} %attention.1.res_ref, bf16[512,1024]{1,0:T(8,128)(2,1)} %wg_ref.1, bf16[512,1024]{1,0:T(8,128)(2,1)} %wu_ref.1, bf16[1024,512]{1,0:T(8,128)(2,1)} %wd_ref.1, ...), custom_call_target="tpu_custom_call" | custom-call | tf_op jit(solution)/shard_map/finish/pallas_call | solution.py:465
  130.5 3.0 %copy.21 = bf16[2048,512]{1,0:T(8,128)(2,1)} copy(bf16[2048,512]{1,0:T(8,128)(2,1)} %finish.1) | data formatting | bytes 4194304

commit v5 on v4

--- a/solution.py
+++ b/solution.py
@@ -20,9 +20,9 @@
 EACH = 32
 CK = BALL // POOL
 NB = ROWS // BALL
-STRIDE = 13
+STRIDE = 37
 LAG = 16
-INVERSE = 5
+INVERSE = 45
 CHIPS = PEERS // 2
 MESH = pl.DeviceIdType.MESH
 F32 = jnp.float32
@@ -280,28 +280,34 @@
         pl.semaphore_signal(barrier, inc=1, device_id={"pts": d}, device_id_type=MESH)
     pl.semaphore_wait(barrier, 3)
 
-    def block(slot):
-        return cand.at[pl.ds(slot * NB, NB)]
-
-    def remote(src, slot, at, d):
-        return pltpu.make_async_remote_copy(
-            src_ref=src, dst_ref=block(slot), send_sem=send.at[at], recv_sem=recv.at[at],
-            device_id={"pts": d}, device_id_type=MESH)
+    half = NB // 2
 
     def slot(e):
         return (2 - e) * 2 + core
 
-    outs = [remote(pooled_ref, slot(e), 1 + i, chip_at(e)) for i, e in enumerate((1, -1))]
-    for copy in outs:
+    def part(at, h):
+        return cand.at[pl.ds(at * NB + h * half, half)]
+
+    def remote(src, at, h, sem, d):
+        return pltpu.make_async_remote_copy(
+            src_ref=src, dst_ref=part(at, h), send_sem=send.at[sem], recv_sem=recv.at[sem],
+            device_id={"pts": d}, device_id_type=MESH)
+
+    def mine(h):
+        return pooled_ref.at[pl.ds(h * half, half)]
+
+    sides = (1, -1)
+    outs = [[remote(mine(h), slot(e), h, h * 2 + i, chip_at(e)) for i, e in enumerate(sides)]
+            for h in range(2)]
+    farther = [[remote(part(slot(e), h), slot(2 * e), h, 4 + h * 2 + i, chip_at(e))
+                for i, e in enumerate(sides)] for h in range(2)]
+    onward = [[remote(part(slot(e), h), slot(e), h, 8 + h * 4 + i, partner)
+               for i, e in enumerate((1, -1, 2, -2))] for h in range(2)]
+    to_partner = [remote(mine(h), slot(0), h, 16 + h, partner) for h in range(2)]
+    for copy in outs[0] + outs[1] + to_partner:
         copy.start()
-    to_partner = remote(pooled_ref, slot(0), 0, partner)
-    to_partner.start()
-    own = pltpu.make_async_copy(pooled_ref, block(slot(0)), here.at[0])
+    own = pltpu.make_async_copy(pooled_ref, cand.at[pl.ds(slot(0) * NB, NB)], here.at[0])
     own.start()
-    farther = [remote(block(slot(e)), slot(2 * e), 3 + i, chip_at(e))
-               for i, e in enumerate((1, -1))]
-    onward = [remote(block(slot(e)), slot(e), 5 + i, partner)
-              for i, e in enumerate((1, -1, 2, -2))]
 
     spread[...] = jnp.zeros_like(spread)
     wqv_t[:D, :] = wq_ref[...].T
@@ -310,18 +316,20 @@
     mix[...] = block_ones(256, HD, HD, 1.0 / HD)
 
     def near(ball, carry):
-        @pl.when(ball == 4)
-        def _():
-            for i in range(2):
-                outs[i].wait_recv()
-                farther[i].start()
-                onward[i].start()
-
-        @pl.when(ball == 7)
-        def _():
-            for i in range(2):
-                farther[i].wait_recv()
-                onward[2 + i].start()
+        for h, at in enumerate((3, 4)):
+            @pl.when(ball == at)
+            def _():
+                for i in range(2):
+                    outs[h][i].wait_recv()
+                    farther[h][i].start()
+                    onward[h][i].start()
+
+        for h, at in enumerate((6, 7)):
+            @pl.when(ball == at)
+            def _():
+                for i in range(2):
+                    farther[h][i].wait_recv()
+                    onward[h][2 + i].start()
 
         rows = pl.ds(pl.multiple_of(ball * BALL, BALL), BALL)
         normed = normed_ref[rows, :]
@@ -343,11 +351,12 @@
 
     lax.fori_loop(0, NB, near, 0)
     own.wait()
-    to_partner.wait()
-    for copy in outs + farther:
-        copy.wait_send()
-    for copy in onward:
-        copy.wait()
+    for h in range(2):
+        to_partner[h].wait()
+        for copy in outs[h] + farther[h]:
+            copy.wait_send()
+        for copy in onward[h]:
+            copy.wait()
 
     def far(ball, carry):
         rows = pl.ds(pl.multiple_of(ball * BALL, BALL), BALL)
@@ -388,8 +397,8 @@
             pltpu.VMEM((2 * D, D), BF16),
             pltpu.VMEM((D, D), BF16),
             pltpu.VMEM((256, 256), BF16),
-            pltpu.SemaphoreType.DMA((9,)),
-            pltpu.SemaphoreType.DMA((9,)),
+            pltpu.SemaphoreType.DMA((18,)),
+            pltpu.SemaphoreType.DMA((18,)),
             pltpu.SemaphoreType.DMA((1,)),
         ],
         compiler_params=pltpu.CompilerParams(

time: 134 us -> 128 us (0.955)
  Pallas kernels: 129 us -> 124 us
    pallas_call x1, Pallas kernels: 42.6 us -> 38.5 us  [finish(): pl.pallas_call(finish_kernel, in_specs=vmem(len(arrays)), out_specs=vmem(...]
    pallas_call x1, Pallas kernels: 48.8 us -> 46.6 us  [front(): pl.pallas_call(front_kernel, in_specs=vmem(3), out_specs=vmem(5), out_sha...]
where the time goes in v5:
time: 128 us
  Pallas kernels  124 us (97%)
  local copies, waits for them, and re-layouts  3.8 us (3%)
    pallas_call x1, Pallas kernels, front(): pl.pallas_call(front_kernel, in_specs=vmem(3), out_specs=vmem(5), out_sha...  46.6 us
    pallas_call x1, Pallas kernels, attention(): pl.pallas_call(attention_kernel, in_specs=[pl.BlockSpec(memory_space=pltp...  38.6 us
    pallas_call x1, Pallas kernels, finish(): pl.pallas_call(finish_kernel, in_specs=vmem(len(arrays)), out_specs=vmem(...  38.5 us
    unnamed x2, local copies, waits for them, and re-layouts  3.8 us

profile of v5, /device:TPU:1, one launch (start us, length us, event | category | flops | bytes accessed | tf_op | source)
XLA Modules:
  0.0 128.2 jit_solution(7887521729522965426)
XLA Ops:
  0.0 0.8 copy.16
  0.8 0.6 fusion.6.chosen_ref
  1.4 46.6 %front.1 = (bf16[2048,512]{1,0:T(8,128)(2,1)}, bf16[2048,512]{1,0:T(8,128)(2,1)}, bf16[8,32,512]{2,1,0:T(8,128)(2,1)}, s32[1,2048]{1,0:T(1,128)}, s32[8,1,256]{2,1,0:T(1,128)}) custom-call(s32[1,2048]{1,0:T(1,128)} %bitcast.3, bf16[2048,512]{1,0:T(8,128)(2,1)} %x_ref.1, f32[1,512]{1,0:T(1,128)} %bitcast.4), custom_call_target="tpu_custom_call" | custom-call | tf_op jit(solution)/shard_map/front/pallas_call | solution.py:200
  48.0 38.6 %attention.1.res_ref = bf16[2048,512]{1,0:T(8,128)(2,1)} custom-call(s32[8,4]{1,0:T(8,128)} %fusion.6.chosen_ref, f32[16]{0:T(128)} %scale_ref.1, bf16[2048,512]{1,0:T(8,128)(2,1)} %get-tuple-element.12.normed_ref, bf16[2048,512]{1,0:T(8,128)(2,1)} %get-tuple-element.13.grouped_ref, bf16[8,32,512]{2,1,0:T(8,128)(2,1)} %get-tuple-element.14.pooled_ref, ...), custom_call_target="tpu_custom_call" | custom-call | tf_op jit(solution)/shard_map/attention/pallas_call | solution.py:385
  86.6 38.5 %finish.1 = bf16[2048,512]{1,0:T(8,128)(2,1)} custom-call(s32[8,1,256]{2,1,0:T(1,128)} %get-tuple-element.10.slot_ref, s32[1,2048]{1,0:T(1,128)} %get-tuple-element.11.pos_ref, bf16[2048,512]{1,0:T(8,128)(2,1)} %attention.1.res_ref, bf16[512,1024]{1,0:T(8,128)(2,1)} %wg_ref.1, bf16[512,1024]{1,0:T(8,128)(2,1)} %wu_ref.1, bf16[1024,512]{1,0:T(8,128)(2,1)} %wd_ref.1, ...), custom_call_target="tpu_custom_call" | custom-call | tf_op jit(solution)/shard_map/finish/pallas_call | solution.py:474
  125.2 3.0 %copy.21 = bf16[2048,512]{1,0:T(8,128)(2,1)} copy(bf16[2048,512]{1,0:T(8,128)(2,1)} %finish.1) | data formatting | bytes 4194304

commit v6 on v5

--- a/solution.py
+++ b/solution.py
@@ -124,8 +124,10 @@
         ids(k).start()
         rows(k).start()
 
-    def prepare(c):
+    def prepare(c, between=None):
         hot = one_hot_rows(c * 256, 256, pos_ref[...])
+        if between is not None:
+            between()
         ready[pl.ds(pl.multiple_of(c * 8, 8), 8)] = mm(hot, x_ref[...]).astype(BF16).reshape(
             8, EACH, D)
         back = mm_nt(parts, hot)
@@ -139,9 +141,8 @@
     own_ids = pltpu.make_async_copy(numbers.at[0], landed_numbers.at[0], here.at[1])
 
     def more(c):
-        prepare(c)
         first = c * 8 - 8
-        steps(jnp.maximum(first, 1), first + 8, start)
+        prepare(c, lambda: steps(jnp.maximum(first, 1), first + 8, start))
 
     steps(1, NB, more)
     own.start()

time: 128 us -> 127 us (level)
  no operation moved by 1% of the time
where the time goes in v6:
time: 127 us
  Pallas kernels  123 us (97%)
  local copies, waits for them, and re-layouts  3.8 us (3%)
    pallas_call x1, Pallas kernels, front(): pl.pallas_call(front_kernel, in_specs=vmem(3), out_specs=vmem(5), out_sha...  45.7 us
    pallas_call x1, Pallas kernels, finish(): pl.pallas_call(finish_kernel, in_specs=vmem(len(arrays)), out_specs=vmem(...  38.5 us
    pallas_call x1, Pallas kernels, attention(): pl.pallas_call(attention_kernel, in_specs=[pl.BlockSpec(memory_space=pltp...  38.5 us
    unnamed x2, local copies, waits for them, and re-layouts  3.8 us

profile of v6, /device:TPU:1, one launch (start us, length us, event | category | flops | bytes accessed | tf_op | source)
XLA Modules:
  0.0 127.3 jit_solution(12440062377069692804)
XLA Ops:
  0.0 0.8 copy.16
  0.8 0.6 fusion.6.chosen_ref
  1.4 45.7 %front.1 = (bf16[2048,512]{1,0:T(8,128)(2,1)}, bf16[2048,512]{1,0:T(8,128)(2,1)}, bf16[8,32,512]{2,1,0:T(8,128)(2,1)}, s32[1,2048]{1,0:T(1,128)}, s32[8,1,256]{2,1,0:T(1,128)}) custom-call(s32[1,2048]{1,0:T(1,128)} %bitcast.3, bf16[2048,512]{1,0:T(8,128)(2,1)} %x_ref.1, f32[1,512]{1,0:T(1,128)} %bitcast.4), custom_call_target="tpu_custom_call" | custom-call | tf_op jit(solution)/shard_map/front/pallas_call | solution.py:201
  47.1 38.5 %attention.1.res_ref = bf16[2048,512]{1,0:T(8,128)(2,1)} custom-call(s32[8,4]{1,0:T(8,128)} %fusion.6.chosen_ref, f32[16]{0:T(128)} %scale_ref.1, bf16[2048,512]{1,0:T(8,128)(2,1)} %get-tuple-element.12.normed_ref, bf16[2048,512]{1,0:T(8,128)(2,1)} %get-tuple-element.13.grouped_ref, bf16[8,32,512]{2,1,0:T(8,128)(2,1)} %get-tuple-element.14.pooled_ref, ...), custom_call_target="tpu_custom_call" | custom-call | tf_op jit(solution)/shard_map/attention/pallas_call | solution.py:386
  85.7 38.5 %finish.1 = bf16[2048,512]{1,0:T(8,128)(2,1)} custom-call(s32[8,1,256]{2,1,0:T(1,128)} %get-tuple-element.10.slot_ref, s32[1,2048]{1,0:T(1,128)} %get-tuple-element.11.pos_ref, bf16[2048,512]{1,0:T(8,128)(2,1)} %attention.1.res_ref, bf16[512,1024]{1,0:T(8,128)(2,1)} %wg_ref.1, bf16[512,1024]{1,0:T(8,128)(2,1)} %wu_ref.1, bf16[1024,512]{1,0:T(8,128)(2,1)} %wd_ref.1, ...), custom_call_target="tpu_custom_call" | custom-call | tf_op jit(solution)/shard_map/finish/pallas_call | solution.py:475
  124.2 3.0 %copy.21 = bf16[2048,512]{1,0:T(8,128)(2,1)} copy(bf16[2048,512]{1,0:T(8,128)(2,1)} %finish.1) | data formatting | bytes 4194304
